TPU v7x, 256 devices: a whole 4x4x8 slice. The times are simulated.
256 devices in a mesh: dp: 8 (over y, core), tensor: 32 (over x, z).
Axes of the slice: x: 4, y: 4, z: 8, core: 2. Of those that a mesh axis runs over, the one named last changes fastest.
Arguments:
- tokens: bfloat16 [2048, 8192], P('dp', 'tensor'), may hold values from -6 to 6
- pattern: int32 [256, 8], P('tensor'), may hold values from 0 to 63, as said below
- first_blocks: bfloat16 [256, 8, 128, 128], P('tensor'), may hold values from -0.1875 to 0.1875
- second_blocks: bfloat16 [256, 8, 128, 128], P('tensor'), may hold values from -0.1875 to 0.1875
- out_grad: bfloat16 [2048, 8192], P('dp', 'tensor'), may hold values from -0.75 to 0.75
Outputs:
- layer_out: bfloat16 [2048, 8192], P('dp', 'tensor')
- input_grad: bfloat16 [2048, 8192], P('dp', 'tensor')
- first_grad: bfloat16 [256, 8, 128, 128], P('tensor')
- second_grad: bfloat16 [256, 8, 128, 128], P('tensor')
Inputs may be any that keep to these rules, and one draw needn't show every extreme that they name: `pattern`: each hidden block row r lists 8 distinct feature blocks: r mod 64, the blocks that differ from it in bit 0, in bit 3 and in the highest bit, and 4 further ones drawn at random. Every feature block is listed by some row.
All inputs are finite; a program needn't handle non-finite values.
Results may differ from a plain program's by a relative error of at most 0.015.
Values may be sent and summed in bfloat16 or wider, within the bound.
A program may use at most 128 MiB of HBM per device.

v0:
```python
import jax
import jax.numpy as jnp
from jax import lax
from jax.sharding import PartitionSpec as P

gelu_scale = 0.7978845608028654
gelu_cube = 0.044715


def gelu_pair(value):
    inner = gelu_scale * (value + gelu_cube * value * value * value)
    tangent = jnp.tanh(inner)
    result = 0.5 * value * (1.0 + tangent)
    slope = 0.5 * (1.0 + tangent) + 0.5 * value * (1.0 - tangent * tangent) * gelu_scale * (
        1.0 + 3.0 * gelu_cube * value * value
    )
    return (result, slope)


def place_blocks(terms, pattern, count):
    targets = jnp.arange(count, dtype=jnp.int32)
    select = (pattern[:, :, None] == targets[None, None, :]).astype(jnp.float32)
    return jnp.einsum("trkc,rkf->ftc", terms, select, precision=lax.Precision.HIGHEST)


def shards(tokens, pattern, first_blocks, second_blocks, out_grad):
    tok_rows = tokens.shape[0]
    block_size = first_blocks.shape[-1]
    group_size = lax.axis_size("tensor")
    feat_blocks = tokens.shape[1] * group_size // block_size
    own_blocks = feat_blocks // group_size
    full_tokens = lax.all_gather(tokens, "tensor", axis=1, tiled=True).reshape(
        tok_rows, feat_blocks, block_size
    )
    picked = full_tokens[:, pattern, :]
    pre = jnp.einsum("trki,rkio->tro", picked, first_blocks, preferred_element_type=jnp.float32)
    value, slope = gelu_pair(pre)
    active = value.astype(jnp.bfloat16)
    contrib = jnp.einsum(
        "tro,rkoc->trkc", active, second_blocks, preferred_element_type=jnp.float32
    )
    out_terms = place_blocks(contrib, pattern, feat_blocks)
    out_rows = lax.psum_scatter(
        out_terms.astype(jnp.bfloat16), "tensor", scatter_dimension=0, tiled=True
    ).astype(jnp.float32)
    layer_out = (
        jnp.transpose(out_rows, (1, 0, 2))
        .reshape(tok_rows, own_blocks * block_size)
        .astype(jnp.bfloat16)
    )
    full_grad = lax.all_gather(out_grad, "tensor", axis=1, tiled=True).reshape(
        tok_rows, feat_blocks, block_size
    )
    grad_picked = full_grad[:, pattern, :]
    second_term = jnp.einsum(
        "tro,trkc->rkoc", active, grad_picked, preferred_element_type=jnp.float32
    )
    act_grad = jnp.einsum(
        "trkc,rkoc->tro", grad_picked, second_blocks, preferred_element_type=jnp.float32
    )
    pre_grad = (act_grad * slope).astype(jnp.bfloat16)
    first_term = jnp.einsum("trki,tro->rkio", picked, pre_grad, preferred_element_type=jnp.float32)
    back_term = jnp.einsum(
        "tro,rkio->trki", pre_grad, first_blocks, preferred_element_type=jnp.float32
    )
    back_terms = place_blocks(back_term, pattern, feat_blocks)
    back_rows = lax.psum_scatter(
        back_terms.astype(jnp.bfloat16), "tensor", scatter_dimension=0, tiled=True
    ).astype(jnp.float32)
    input_grad = (
        jnp.transpose(back_rows, (1, 0, 2))
        .reshape(tok_rows, own_blocks * block_size)
        .astype(jnp.bfloat16)
    )
    first_total, second_total = (
        lax.psum(first_term.astype(jnp.bfloat16), "dp").astype(jnp.float32),
        lax.psum(second_term.astype(jnp.bfloat16), "dp").astype(jnp.float32),
    )
    first_grad = first_total.astype(jnp.bfloat16)
    second_grad = second_total.astype(jnp.bfloat16)
    return (layer_out, input_grad, first_grad, second_grad)


def solution(mesh):
    placed = (
        P("dp", "tensor"),
        P("tensor", None),
        P("tensor", None, None, None),
        P("tensor", None, None, None),
        P("dp", "tensor"),
    )
    return jax.shard_map(
        shards,
        mesh=mesh,
        in_specs=placed,
        out_specs=(
            P("dp", "tensor"),
            P("dp", "tensor"),
            P("tensor", None, None, None),
            P("tensor", None, None, None),
        ),
        check_vma=False,
    )
```

profile of v0, /device:TPU:1, one launch (start us, length us, event | category | flops | bytes accessed | tf_op | source)
XLA Modules:
  0.0 753.5 jit_solution(4094566455043544429)
XLA Ops:
  7.2 0.0 copy-start
  7.2 0.0 all-gather.3.cloned.1.call-start
  7.2 1.8 copy.48
  9.0 0.0 all-gather.3.cloned.1.call-update
  9.1 0.0 all-gather.5.cloned.1.call-start
  9.1 1.7 copy.55
  10.8 0.0 all-gather.5.cloned.1.call-update
  10.8 0.0 all-reduce.3.cloned.1.call-start
  10.8 0.7 compare_select_fusion
  11.5 0.1 reshape.23
  11.6 81.5 %all-gather.3.cloned.1.call-done = bf16[256,8192]{0,1:T(8,128)(2,1)} async-done(((bf16[256,256]{0,1:T(8,128)(2,1)}), bf16[256,8192]{0,1:T(8,128)(2,1)}) %all-gather.3.cloned.1.call-update) | async-done | bytes 4194320 | tf_op jit(solution)/shard_map/all_gather | solution.py:32
  93.2 6.4 copy.49
  99.6 75.3 %all-gather.5.cloned.1.call-done = bf16[256,8192]{0,1:T(8,128)(2,1)} async-done(((bf16[256,256]{0,1:T(8,128)(2,1)}), bf16[256,8192]{0,1:T(8,128)(2,1)}) %all-gather.5.cloned.1.call-update) | async-done | bytes 4194320 | tf_op jit(solution)/shard_map/all_gather | solution.py:51
  174.8 6.4 copy.56
  181.2 5.2 gather_fusion
  186.5 5.2 gather_fusion.1
  191.7 6.4 copy.57
  198.1 6.5 copy.50
  204.6 0.0 copy-start.4
  204.6 4.2 convolution_bitcast_fusion.3
  208.8 0.0 copy-done.4
  208.9 0.0 copy-start.2
  208.9 2.6 convert_bitcast_fusion
  211.5 0.0 copy-done
  211.5 0.0 copy-done.2
  211.5 0.0 copy-start.3
  211.5 1.3 fusion.19
  212.8 0.0 copy-start.6
  212.8 0.8 copy-done.6
  213.6 0.1 copy-done.3
  213.7 0.0 copy-start.8
  213.7 2.6 fusion.12
  216.3 0.0 all-reduce.3.cloned.1.call-update
  216.3 0.2 reduce-scatter.3.cloned.1.call-start
  216.5 0.0 copy-done.8
  216.6 0.1 copy.47
  216.6 1.2 convolution_bitcast_fusion.1
  217.9 12.1 %bitcast_convert_fusion.1 = bf16[64,256,128]{2,0,1:T(8,128)(2,1)S(1)} fusion(f32[256,8,8,128]{3,0,2,1:T(8,128)S(1)} %convolution_bitcast_fusion.1, s32[8,8]{0,1:T(8,128)S(1)} %copy.47), kind=kOutput, calls=%fused_computation.3 | convolution fusion | flops 1612713984 | bytes 12583168 | tf_op jit(solution)/shard_map/trkc,rkf->ftc/dot_general | solution.py:23
  230.0 4.7 copy.53
  234.7 0.0 copy-start.5
  234.7 0.0 copy-start.7
  234.7 0.0 reduce-scatter.3.cloned.1.call-update
  234.7 0.3 reduce-scatter.5.cloned.1.call-start
  235.0 1.3 copy-done.5
  236.3 0.1 copy-done.7
  236.4 1.2 convolution_bitcast_fusion
  237.7 12.1 %bitcast_convert_fusion = bf16[64,256,128]{2,0,1:T(8,128)(2,1)S(1)} fusion(f32[256,8,8,128]{3,0,2,1:T(8,128)S(1)} %convolution_bitcast_fusion, s32[8,8]{0,1:T(8,128)S(1)} %copy.47), kind=kOutput, calls=%fused_computation.2 | convolution fusion | flops 1612713984 | bytes 12583168 | tf_op jit(solution)/shard_map/trkc,rkf->ftc/dot_general | solution.py:23
  249.8 4.7 copy.60
  254.5 0.0 reduce-scatter.5.cloned.1.call-update
  254.5 38.2 %all-reduce.3.cloned.1.call-done = (bf16[8,8,128,128]{3,2,1,0:T(8,128)(2,1)}, bf16[8,8,128,128]{2,3,1,0:T(8,128)(2,1)}) async-done(((bf16[8,8,128,128]{3,2,1,0:T(8,128)(2,1)}, bf16[8,8,128,128]{2,3,1,0:T(8,128)(2,1)}), (bf16[8,8,128,128]{3,2,1,0:T(8,128)(2,1)}, bf16[8,8,128,128]{2,3,1,0:T(8,128)(2,1)})) %all-reduce.3.cloned.1.call-update) | async-done | bytes 4194320 | tf_op jit(solution)/shard_map/psum | solution.py:76
  292.7 0.0 copy-start.1
  292.7 4.1 copy.64
  296.8 219.8 %reduce-scatter.3.cloned.1.call-done = bf16[2,256,128]{2,1,0:T(8,128)(2,1)} async-done(((bf16[64,256,128]{2,1,0:T(8,128)(2,1)}), bf16[2,256,128]{2,1,0:T(8,128)(2,1)}) %reduce-scatter.3.cloned.1.call-update) | async-done | bytes 131088 | tf_op jit(solution)/shard_map/reduce_scatter | solution.py:43
  516.6 1.0 copy.54
  517.6 0.8 copy.62
  518.4 223.7 %reduce-scatter.5.cloned.1.call-done = bf16[2,256,128]{2,1,0:T(8,128)(2,1)} async-done(((bf16[64,256,128]{2,1,0:T(8,128)(2,1)}), bf16[2,256,128]{2,1,0:T(8,128)(2,1)}) %reduce-scatter.5.cloned.1.call-update) | async-done | bytes 131088 | tf_op jit(solution)/shard_map/reduce_scatter | solution.py:67
  742.1 1.0 copy.61
  743.1 0.8 copy.63
  743.8 3.2 copy.87
  747.0 0.0 copy-done.1
  (1 shorter events, 0.0 us)
Async XLA Ops:
  7.2 204.3 %copy-start = (bf16[8,8,128,128]{3,2,1,0:T(8,128)(2,1)S(1)}, bf16[8,8,128,128]{3,2,1,0:T(8,128)(2,1)}, u32[]{:S(2)}) copy-start(bf16[8,8,128,128]{3,2,1,0:T(8,128)(2,1)} %param.8) | copy-start | bytes 6291460
  7.2 86.0 %all-gather.3.cloned.1.call-start = ((), (), s32[]{:S(2)}) async-start(), calls=%async_computation.2 | async-start | bytes 4325376 | tf_op jit(solution)/shard_map/all_gather | solution.py:32
  9.1 165.8 %all-gather.5.cloned.1.call-start = ((), (), s32[]{:S(2)}) async-start(), calls=%async_computation.4 | async-start | bytes 4325376 | tf_op jit(solution)/shard_map/all_gather | solution.py:51
  10.8 281.9 %all-reduce.3.cloned.1.call-start = ((), (), s32[]{:S(2)}) async-start(), calls=%async_computation.6 | async-start | bytes 8388608 | tf_op jit(solution)/shard_map/psum | solution.py:76
  204.6 4.3 copy-start.4
  208.9 2.7 copy-start.2
  211.5 2.2 copy-start.3
  212.8 0.8 copy-start.6
  213.7 2.8 copy-start.8
  216.3 300.3 %reduce-scatter.3.cloned.1.call-start = ((), (), s32[]{:S(2)}) async-start(), calls=%async_computation.3 | async-start | bytes 4325376 | tf_op jit(solution)/shard_map/reduce_scatter | solution.py:43
  234.7 1.6 copy-start.5
  234.7 1.7 copy-start.7
  234.7 507.4 %reduce-scatter.5.cloned.1.call-start = ((), (), s32[]{:S(2)}) async-start(), calls=%async_computation.5 | async-start | bytes 4325376 | tf_op jit(solution)/shard_map/reduce_scatter | solution.py:67
  292.7 454.3 %copy-start.1 = (bf16[8,8,128,128]{3,2,1,0:T(8,128)(2,1)S(1)}, bf16[8,8,128,128]{3,2,1,0:T(8,128)(2,1)}, u32[]{:S(2)}) copy-start(bf16[8,8,128,128]{3,2,1,0:T(8,128)(2,1)} %param.8) | copy-start | bytes 6291460
Sparse Core Ops, SparseCore 0:
  11.2 81.9 all-gather.2
  96.3 78.4 all-gather.4
  216.4 76.2 all-reduce.2
  296.4 220.1 reduce-scatter.2
  520.3 221.6 reduce-scatter.4
where the time goes:
time: 759 us; the launch traced here: 754 us
  waiting for transfers between devices  639 us (84%)
  local copies, waits for them, and re-layouts  62.2 us (8%)
  matrix products  37.5 us (5%)
  between operations  13.9 us (2%)
    reduce_scatter x1, waiting for transfers between devices, shards(): lax.psum_scatter(back_terms.astype(jnp.bfloat16), 'tensor', scatter_dimen...  224 us
    reduce_scatter x1, waiting for transfers between devices, shards(): lax.psum_scatter(out_terms.astype(jnp.bfloat16), 'tensor', scatter_dimens...  220 us
    all_gather x1, waiting for transfers between devices, shards(): lax.all_gather(tokens, 'tensor', axis=1, tiled=True)  81.5 us
    all_gather x1, waiting for transfers between devices, shards(): lax.all_gather(out_grad, 'tensor', axis=1, tiled=True)  75.3 us
    psum x1, waiting for transfers between devices, shards(): lax.psum(first_term.astype(jnp.bfloat16), 'dp').astype(jnp.float32)  38.2 us
    dot_general x2, matrix products, place_blocks(): jnp.einsum('trkc,rkf->ftc', terms, select, precision=lax.Precision.HIGHEST)  24.3 us
  transfers between devices with their start and end apart: 5, of which 5 were waited for; matrix products, arithmetic and copies ran while one was open for 7% of the time, Pallas kernels for 0%

commit v1 on v0

v1 whole, which is shorter than its diff:
```python
import heapq

import jax
import jax.numpy as jnp
from jax import lax
from jax.experimental import pallas as pl
from jax.experimental.pallas import tpu as pltpu
from jax.sharding import PartitionSpec as P

MESH = pl.DeviceIdType.MESH
BF = jnp.bfloat16
F32 = jnp.float32

gelu_scale = 0.7978845608028654
gelu_cube = 0.044715

NX, NZ, NY = 4, 8, 4
ROWS, BLK, HR, K = 256, 128, 8, 8
RA = 96
RB = ROWS - RA
SIGNS = (1, -1)


UNIT = 2.8
LAT = 1.6
GB2 = UNIT


def build_items():
    items = {}

    def add(key, link, size, deps):
        items[key] = (link, size, tuple(deps))

    fa, fb = RA / ROWS, RB / ROWS

    def name(axis, s):
        return axis + ("+" if s > 0 else "-")

    for p in (0, 1):
        gate = [("gate", "ag", p)]
        for s in SIGNS:
            add(("bz", p, s, 1), name("z", s), fb, gate)
            add(("ax", p, s, 1), name("x", s), fa, gate)
        for s in SIGNS:
            add(("az", p, 0, s, 1), name("z", s), fa, gate)
            add(("bx", p, 0, s, 1), name("x", s), fb, gate)
        for s in SIGNS:
            add(("ax", p, s, 2), name("x", s), fa / 2, [("ax", p, s, 1)])
            for k in (2, 3, 4):
                add(("bz", p, s, k), name("z", s), fb if k < 4 else fb / 2, [("bz", p, s, k - 1)])
        for dx, ready in (
            (0, gate),
            (-1, [("ax", p, 1, 1)]),
            (1, [("ax", p, -1, 1)]),
            (2, [("ax", p, 1, 2), ("ax", p, -1, 2)]),
        ):
            for s in SIGNS:
                for k in (1, 2, 3, 4):
                    add(
                        ("az", p, dx, s, k),
                        name("z", s),
                        fa if k < 4 else fa / 2,
                        ready if k == 1 else [("az", p, dx, s, k - 1)],
                    )
        for dz in (0, -1, 1, -2, 2, -3, 3, 4):
            if dz == 0:
                ready = gate
            elif dz == 4:
                ready = [("bz", p, 1, 4), ("bz", p, -1, 4)]
            else:
                ready = [("bz", p, 1 if dz < 0 else -1, abs(dz))]
            for s in SIGNS:
                add(("bx", p, dz, s, 1), name("x", s), fb, ready)
                add(("bx", p, dz, s, 2), name("x", s), fb / 2, [("bx", p, dz, s, 1)])
    for q in (0, 1):
        gate = [("gate", "rs", q)]

        def done_a(dx):
            return [("rz", q, dx, s, 1) for s in SIGNS]

        def done_b(dz):
            return [("sx", q, dz, s, 1) for s in SIGNS]

        for dx in (2, 1, -1, 0):
            for s in SIGNS:
                for k in (4, 3, 2, 1):
                    add(
                        ("rz", q, dx, s, k),
                        name("z", s),
                        fa if k < 4 else fa / 2,
                        gate if k == 4 else [("rz", q, dx, s, k + 1)],
                    )
        for dz in (4, 3, -3, 2, -2, 1, -1, 0):
            for s in SIGNS:
                add(("sx", q, dz, s, 2), name("x", s), fb / 2, gate)
                add(("sx", q, dz, s, 1), name("x", s), fb, [("sx", q, dz, s, 2)])
        for s in SIGNS:
            add(("rx", q, s, 2), name("x", s), fa / 2, done_a(2))
            add(("rx", q, s, 1), name("x", s), fa, [("rx", q, s, 2)] + done_a(s))
            add(("sz", q, s, 4), name("z", s), fb / 2, done_b(4))
            for k in (3, 2, 1):
                add(("sz", q, s, k), name("z", s), fb, [("sz", q, s, k + 1)] + done_b(s * k))
    for m in (0, 1):
        add(("pc", m), "c", 1.6, [("grad", m)])
        for s in SIGNS:
            add(("yr", m, s, 2), name("y", s), 1.0, [("pc", m)])
            add(("yr", m, s, 1), name("y", s), 2.0, [("yr", m, s, 2)])
        fin = [("yr", m, s, 1) for s in SIGNS]
        for s in SIGNS:
            add(("yg", m, s, 1), name("y", s), 2.0, fin)
            add(("yg", m, s, 2), name("y", s), 1.0, [("yg", m, s, 1)])
        add(("cg", m, 0), "c", 0.4, fin)
        add(("cg", m, -1), "c", 0.4, [("yg", m, 1, 1)])
        add(("cg", m, 1), "c", 0.4, [("yg", m, -1, 1)])
        add(("cg", m, 2), "c", 0.4, [("yg", m, 1, 2), ("yg", m, -1, 2)])
    return items


def build_chunks(items):
    def all_of(kinds, p):
        return [k for k in items if k[0] in kinds and k[1] == p]

    ag = ("ax", "az", "bz", "bx")
    chunks = [(("load",), 0.5, [("count", "ag", 0, 30)])]
    chunks += [(("pre", i), 1.5, all_of(ag, 0) + [("load",)]) for i in range(4)]
    pre = [("pre", i) for i in range(4)]
    chunks += [(("out", i), 1.0, pre) for i in range(8)]
    chunks += [(("sterm", i), 1.2, all_of(ag, 1) + pre) for i in range(4)]
    chunks += [(("agrad", i), 1.5, all_of(ag, 1) + pre) for i in range(4)]
    agr = [("agrad", i) for i in range(4)]
    chunks += [(("fterm", i), 1.4, agr) for i in range(4)]
    chunks += [(("back", i), 1.0, agr) for i in range(8)]
    return chunks


def build_marks(items):
    final = [
        [("rx", q, s, 1) for s in SIGNS]
        + [("rz", q, 0, s, 1) for s in SIGNS]
        + [("sz", q, s, 1) for s in SIGNS]
        + [("sx", q, 0, s, 1) for s in SIGNS]
        for q in (0, 1)
    ]
    marks = [
        (("gate", "ag", 0), []),
        (("gate", "ag", 1), [("count", "ag", 0, 62)]),
        (("gate", "rs", 0), [("out", i) for i in range(8)] + [("count", "ag", 1, 62)]),
        (("gate", "rs", 1), [("back", i) for i in range(8)] + [("count", "rs", 0, 62)]),
        (("grad", 0), [("sterm", i) for i in range(4)]),
        (("grad", 1), [("fterm", i) for i in range(4)]),
        (("store", 0), final[0]),
        (("store", 1), final[1]),
        (("own", 0), [("yr", 0, s, 1) for s in SIGNS]),
        (("own", 1), [("yr", 1, s, 1) for s in SIGNS]),
    ]
    return marks


GROUP = {k: "ag" for k in ("ax", "az", "bz", "bx")} | {k: "rs" for k in ("rz", "rx", "sx", "sz")}
COST = {"ag": 0.03, "rs": 0.15}


def build_order():
    items = build_items()
    chunks = build_chunks(items)
    marks = build_marks(items)
    got, counts, free = set(), {}, {}
    waiting = list(items)
    heap, order = [], []
    now, seq = 0.0, 0

    def met(need):
        if need[0] == "count":
            return counts.get((need[1], need[2]), 0) >= need[3]
        return need in got

    def settle():
        nonlocal now, seq
        moved = True
        while moved:
            moved = False
            for mark in list(marks):
                if all(met(n) for n in mark[1]):
                    marks.remove(mark)
                    order.append(("mark", mark[0]))
                    got.add(mark[0])
                    moved = True
            for key in list(waiting):
                link, size, deps = items[key]
                if all(d in got for d in deps):
                    waiting.remove(key)
                    order.append(("send", key))
                    now += 0.03
                    start = max(now, free.get(link, 0.0))
                    free[link] = start + size * UNIT
                    seq += 1
                    heapq.heappush(heap, (free[link] + LAT, seq, key))
                    moved = True

    settle()
    while heap or chunks:
        if heap and heap[0][0] <= now:
            key = heapq.heappop(heap)[2]
            order.append(("recv", key))
            got.add(key)
            group = GROUP.get(key[0], "ar")
            counts[(group, key[1])] = counts.get((group, key[1]), 0) + 1
            now += COST.get(group, 0.3)
            settle()
            continue
        if chunks and all(met(n) for n in chunks[0][2]):
            key, time, _ = chunks.pop(0)
            order.append(("comp", key))
            got.add(key)
            now += time
            settle()
            continue
        now = max(now, heap[0][0])
    assert not waiting and not marks
    return list(items), order, now


KEYS, ORDER, SPAN = build_order()
INDEX = {k: i for i, k in enumerate(KEYS)}


def slot_index():
    a, b, y = {}, {}, {}
    for k in KEYS:
        if k[0] in ("rz", "rx") and k[1] == 0:
            a[(k[0],) + k[2:]] = len(a)
        if k[0] in ("sx", "sz") and k[1] == 0:
            b[(k[0],) + k[2:]] = len(b)
        if k[0] == "yr" and k[1] == 0:
            y[k[2:]] = len(y)
    return a, b, y


SLOT_A, SLOT_B, SLOT_Y = slot_index()


def gelu_pair(value):
    inner = gelu_scale * (value + gelu_cube * value * value * value)
    tangent = jnp.tanh(inner)
    result = 0.5 * value * (1.0 + tangent)
    slope = 0.5 * (1.0 + tangent) + 0.5 * value * (1.0 - tangent * tangent) * gelu_scale * (
        1.0 + 3.0 * gelu_cube * value * value
    )
    return result, slope


def kernel(
    tokens, grads, patv, pats, first, second,
    out_ref, back_ref, fgrad_ref, sgrad_ref,
    xb, gb, part0, part1, slot_a, slot_b, w1, w2, act, pgrad, slope_ref,
    sgr, fgr, pair, yslot, invv, invs,
    send_sem, recv_sem, local_sem,
):
    t = lax.axis_index("tensor")
    d = lax.axis_index("dp")
    x, z = lax.div(t, NZ), lax.rem(t, NZ)
    y, core = lax.div(d, 2), lax.rem(d, 2)

    def at(dx, dz):
        return lax.rem(x + (dx + NX), NX) * NZ + lax.rem(z + (dz + NZ), NZ)

    def dev_x(s):
        return {"tensor": at(s, 0)}

    def dev_z(s):
        return {"tensor": at(0, s)}

    def dev_y(s):
        return {"dp": lax.rem(y + (s + NY), NY) * 2 + core}

    partner = {"dp": y * 2 + (1 - core)}
    base = core * 4

    def yrow(dy, b=None):
        return (base if b is None else b) + lax.rem(y + (dy + NY), NY)

    barrier = pltpu.get_barrier_semaphore()
    for dev in (dev_x(1), dev_x(-1), dev_z(1), dev_z(-1), dev_y(1), dev_y(-1), partner):
        pl.semaphore_signal(barrier, inc=1, device_id=dev, device_id_type=MESH)

    local = []
    for n, (src, buf) in enumerate(((tokens, xb), (grads, gb))):
        for h in (0, 1):
            c = pltpu.make_async_copy(
                src.at[:, pl.ds(h * BLK, BLK)], buf.at[t, h], local_sem.at[2 * n + h]
            )
            c.start()
            local.append(c)
    load_w1 = pltpu.make_async_copy(first, w1.at[:, pl.ds(0, K)], local_sem.at[4])
    load_w2 = pltpu.make_async_copy(second, w2.at[:, pl.ds(0, K)], local_sem.at[5])
    load_w1.start()
    load_w2.start()

    cols = lax.broadcasted_iota(jnp.int32, (HR, BLK), 1)
    inv = jnp.full((HR, BLK), K, jnp.int32)
    for j in range(K):
        inv = jnp.where(patv[:, j : j + 1] == cols, j, inv)
    invv[...] = inv
    load_inv = pltpu.make_async_copy(invv, invs, local_sem.at[6])
    load_inv.start()
    for c in local:
        c.wait()

    pl.semaphore_wait(barrier, 7)

    gathered = (xb, gb)
    parts = (part0, part1)
    grad_of = (sgr, fgr)
    grad_out = (sgrad_ref, fgrad_ref)
    rows_a, rows_b = pl.ds(0, RA), pl.ds(RA, RB)

    def half(s):
        return 0 if s > 0 else 1

    def copy_of(key, sent=True):
        kind = key[0]
        i = INDEX[key]
        ss, rs = send_sem.at[i], recv_sem.at[i]

        def remote(src, dst, dev):
            return pltpu.make_async_remote_copy(
                src_ref=src, dst_ref=dst, send_sem=ss, recv_sem=rs, device_id=dev, device_id_type=MESH
            )

        if kind in ("ax", "az", "bz", "bx"):
            buf = gathered[key[1]]
            s, k = key[-2], key[-1]
            rows = rows_a if kind[0] == "a" else rows_b
            if kind == "ax":
                own, got, dev, split = at(-s * (k - 1), 0), at(-s * k, 0), dev_x(s), k == 2
            elif kind == "az":
                dx = key[2]
                own, got, dev, split = at(dx, -s * (k - 1)), at(dx, -s * k), dev_z(s), k == 4
            elif kind == "bz":
                own, got, dev, split = at(0, -s * (k - 1)), at(0, -s * k), dev_z(s), k == 4
            else:
                dz = key[2]
                own, got, dev, split = at(-s * (k - 1), dz), at(-s * k, dz), dev_x(s), k == 2
            hs = pl.ds(half(s), 1) if split else pl.ds(0, 2)

            def view(shard):
                return buf.at[shard, hs, rows, :]

            shard = own if sent else got
            return remote(view(shard), view(shard), dev)
        if kind in ("rz", "rx", "sx", "sz"):
            q, s, k = key[1], key[-2], key[-1]
            buf = parts[q]
            sub = (kind,) + key[2:]
            if kind[0] == "r":
                rows, slot = rows_a, slot_a.at[q, SLOT_A[sub]]
            else:
                rows, slot = rows_b, slot_b.at[q, SLOT_B[sub]]
            if kind == "rz":
                own, dev, split = at(key[2], s * k), dev_z(s), k == 4
            elif kind == "sz":
                own, dev, split = at(0, s * k), dev_z(s), k == 4
            elif kind == "rx":
                own, dev, split = at(s * k, 0), dev_x(s), k == 2
            else:
                own, dev, split = at(s * k, key[2]), dev_x(s), k == 2
            hs = pl.ds(half(s), 1) if split else pl.ds(0, 2)
            return remote(buf.at[own, hs, rows, :], slot.at[hs], dev)
        m = key[1]
        g, out = grad_of[m], grad_out[m]
        if kind == "pc":
            return remote(g.at[pl.ds((1 - core) * 4, 4)], pair.at[m], partner)
        if kind == "yr":
            s, k = key[2], key[3]
            js = pl.ds(half(s) * 4, 4) if k == 2 else pl.ds(0, 8)
            return remote(g.at[yrow(s * k), js], yslot.at[m, SLOT_Y[(s, k)], js], dev_y(s))
        if kind == "yg":
            s, k = key[2], key[3]
            js = pl.ds(half(s) * 4, 4) if k == 2 else pl.ds(0, 8)
            if not sent:
                got = out.at[yrow(-s * k), js]
                return remote(got, got, dev_y(s))
            src = g.at[yrow(0), js] if k == 1 else out.at[yrow(-s), js]
            return remote(src, out.at[yrow(-s * (k - 1)), js], dev_y(s))
        dy = key[2]
        if not sent:
            got = out.at[yrow(dy, (1 - core) * 4)]
            return remote(got, got, partner)
        src = g.at[yrow(0)] if dy == 0 else out.at[yrow(dy)]
        return remote(src, out.at[yrow(dy)], partner)

    def received(key):
        kind = key[0]
        copy_of(key, sent=False).wait_recv()
        if kind in ("rz", "rx", "sx", "sz"):
            q, s, k = key[1], key[-2], key[-1]
            buf = parts[q]
            sub = (kind,) + key[2:]
            if kind[0] == "r":
                rows, slot = rows_a, slot_a.at[q, SLOT_A[sub]]
            else:
                rows, slot = rows_b, slot_b.at[q, SLOT_B[sub]]
            if kind == "rz":
                mine, split = at(key[2], s * (k - 1)), k == 4
            elif kind == "sz":
                mine, split = at(0, s * (k - 1)), k == 4
            elif kind == "rx":
                mine, split = at(s * (k - 1), 0), k == 2
            else:
                mine, split = at(s * (k - 1), key[2]), k == 2
            for h in (half(s),) if split else (0, 1):
                total = buf[mine, h, rows, :].astype(F32) + slot[h].astype(F32)
                buf[mine, h, rows, :] = total.astype(BF)
        elif kind == "pc":
            m = key[1]
            g = grad_of[m]

            @pl.loop(0, 4)
            def _(r):
                @pl.loop(0, K)
                def _(j):
                    total = g[base + r, j].astype(F32) + pair[m, r, j].astype(F32)
                    g[base + r, j] = total.astype(BF)
        elif kind == "yr":
            m, s, k = key[1:]
            g = grad_of[m]
            lo, n = (half(s) * 4, 4) if k == 2 else (0, 8)
            row = yrow(s * (k - 1))

            @pl.loop(lo, lo + n)
            def _(j):
                total = g[row, j].astype(F32) + yslot[m, SLOT_Y[(s, k)], j].astype(F32)
                g[row, j] = total.astype(BF)

    def picked(buf, r):
        return jnp.concatenate([buf[lax.div(pats[r, j], 2), lax.rem(pats[r, j], 2)] for j in range(K)], axis=1)

    def whole(ref):
        return jnp.concatenate([ref[r] for r in range(HR)], axis=1)

    nt = (((1,), (1,)), ((), ()))

    def compute(key):
        kind = key[0]
        if kind == "load":
            load_w1.wait()
            load_w2.wait()
            load_inv.wait()
            for w in (w1, w2):
                for r in range(HR):
                    w[r, K] = jnp.zeros((BLK, BLK), BF)
            return
        i = key[1]
        if kind in ("out", "back"):

            @pl.loop(i * 4, i * 4 + 4)
            def _(dest):
                if kind == "out":
                    rhs = jnp.concatenate(
                        [
                            jnp.concatenate([w2[r, invs[r, 2 * dest + h]] for r in range(HR)], axis=0)
                            for h in (0, 1)
                        ],
                        axis=1,
                    )
                    res = jnp.dot(whole(act), rhs, preferred_element_type=F32)
                else:
                    rhs = jnp.concatenate(
                        [
                            jnp.concatenate([w1[r, invs[r, 2 * dest + h]] for r in range(HR)], axis=1)
                            for h in (0, 1)
                        ],
                        axis=0,
                    )
                    res = lax.dot_general(whole(pgrad), rhs, nt, preferred_element_type=F32)
                buf = part0 if kind == "out" else part1
                for h in (0, 1):
                    buf[dest, h] = res[:, h * BLK : (h + 1) * BLK].astype(BF)

            return

        @pl.loop(i * 2, i * 2 + 2)
        def _(r):
            if kind == "pre":
                weights = jnp.concatenate([w1[r, j] for j in range(K)], axis=0)
                pre = jnp.dot(picked(xb, r), weights, preferred_element_type=F32)
                value, slope = gelu_pair(pre)
                act[r] = value.astype(BF)
                slope_ref[r] = slope
            elif kind == "sterm":
                res = jnp.dot(act[r].T, picked(gb, r), preferred_element_type=F32)
                for j in range(K):
                    sgr[r, j] = res[:, j * BLK : (j + 1) * BLK].astype(BF)
            elif kind == "agrad":
                weights = jnp.concatenate([w2[r, j] for j in range(K)], axis=1)
                res = lax.dot_general(picked(gb, r), weights, nt, preferred_element_type=F32)
                pgrad[r] = (res * slope_ref[r]).astype(BF)
            elif kind == "fterm":
                res = jnp.dot(pgrad[r].T, picked(xb, r), preferred_element_type=F32)
                for j in range(K):
                    fgr[r, j] = res[:, j * BLK : (j + 1) * BLK].astype(BF).T

    stores = []

    def store(src, dst):
        c = pltpu.make_async_copy(src, dst, local_sem.at[8 + len(stores)])
        c.start()
        stores.append(c)

    def marked(key):
        if key[0] == "store":
            q = key[1]
            dst = (out_ref, back_ref)[q]
            for h in (0, 1):
                store(parts[q].at[t, h], dst.at[:, pl.ds(h * BLK, BLK)])
        elif key[0] == "own":
            m = key[1]
            store(grad_of[m].at[yrow(0)], grad_out[m].at[yrow(0)])

    for action, key in ORDER:
        if action == "send":
            copy_of(key).start()
        elif action == "recv":
            received(key)
        elif action == "comp":
            compute(key)
        else:
            marked(key)
    for key in KEYS:
        copy_of(key).wait_send()
    for c in stores:
        c.wait()


def shards(tokens, pattern, first_blocks, second_blocks, out_grad):
    any_space = pl.BlockSpec(memory_space=pl.ANY)
    n = len(KEYS)
    return pl.pallas_call(
        kernel,
        out_shape=(
            jax.ShapeDtypeStruct(tokens.shape, BF),
            jax.ShapeDtypeStruct(tokens.shape, BF),
            jax.ShapeDtypeStruct(first_blocks.shape, BF),
            jax.ShapeDtypeStruct(second_blocks.shape, BF),
        ),
        in_specs=[
            any_space,
            any_space,
            pl.BlockSpec(memory_space=pltpu.VMEM),
            pl.BlockSpec(memory_space=pltpu.SMEM),
            any_space,
            any_space,
        ],
        out_specs=(any_space,) * 4,
        scratch_shapes=[
            pltpu.VMEM((32, 2, ROWS, BLK), BF),
            pltpu.VMEM((32, 2, ROWS, BLK), BF),
            pltpu.VMEM((32, 2, ROWS, BLK), BF),
            pltpu.VMEM((32, 2, ROWS, BLK), BF),
            pltpu.VMEM((2, len(SLOT_A), 2, RA, BLK), BF),
            pltpu.VMEM((2, len(SLOT_B), 2, RB, BLK), BF),
            pltpu.VMEM((HR, K + 1, BLK, BLK), BF),
            pltpu.VMEM((HR, K + 1, BLK, BLK), BF),
            pltpu.VMEM((HR, ROWS, BLK), BF),
            pltpu.VMEM((HR, ROWS, BLK), BF),
            pltpu.VMEM((HR, ROWS, BLK), F32),
            pltpu.VMEM((HR, K, BLK, BLK), BF),
            pltpu.VMEM((HR, K, BLK, BLK), BF),
            pltpu.VMEM((2, 4, K, BLK, BLK), BF),
            pltpu.VMEM((2, 4, K, BLK, BLK), BF),
            pltpu.VMEM((HR, BLK), jnp.int32),
            pltpu.SMEM((HR, BLK), jnp.int32),
            pltpu.SemaphoreType.DMA((n,)),
            pltpu.SemaphoreType.DMA((n,)),
            pltpu.SemaphoreType.DMA((16,)),
        ],
        compiler_params=pltpu.CompilerParams(
            collective_id=0, has_side_effects=True, vmem_limit_bytes=62 * 1024 * 1024
        ),
    )(tokens, out_grad, pattern, pattern, first_blocks, second_blocks)


def solution(mesh):
    placed = (
        P("dp", "tensor"),
        P("tensor", None),
        P("tensor", None, None, None),
        P("tensor", None, None, None),
        P("dp", "tensor"),
    )
    return jax.shard_map(
        shards,
        mesh=mesh,
        in_specs=placed,
        out_specs=(
            P("dp", "tensor"),
            P("dp", "tensor"),
            P("tensor", None, None, None),
            P("tensor", None, None, None),
        ),
        check_vma=False,
    )
```

time: 759 us -> 148 us (0.19)
  waiting for transfers between devices: 639 us -> 0 us
  Pallas kernels: 0 us -> 140 us
  local copies, waits for them, and re-layouts: 62.2 us -> 7.77 us
  matrix products: 37.5 us -> 0 us
  between operations: 13.9 us -> 0.64 us
    reduce_scatter x2 -> x0, waiting for transfers between devices: 444 us -> none  [the longest x1 224 us: shards(): lax.psum_scatter(back_terms.astype(jnp.bfloat16), 'tensor', scatter_dimen...]
    all_gather x2 -> x0, waiting for transfers between devices: 157 us -> none  [the longest x1 81.5 us: shards(): lax.all_gather(tokens, 'tensor', axis=1, tiled=True)]
    pallas_call x0 -> x1, Pallas kernels: none -> 140 us  [shards(): pl.pallas_call(kernel, out_shape=(jax.ShapeDtypeStruct(tokens.shape, BF),...]
    psum x1 -> x0, waiting for transfers between devices: 38.2 us -> none  [shards(): lax.psum(first_term.astype(jnp.bfloat16), 'dp').astype(jnp.float32)]
    dot_general x8 -> x0, matrix products: 37.5 us -> none  [the longest x2 24.3 us: place_blocks(): jnp.einsum('trkc,rkf->ftc', terms, select, precision=lax.Precision.HIGHEST)]
    gather x4 -> x0, local copies, waits for them, and re-layouts: 23.4 us -> none  [the longest x2 11.7 us: shards(): grad_picked = full_grad[:, pattern, :]]
    reshape x2 -> x0, local copies, waits for them, and re-layouts: 12.8 us -> none  [the longest x1 6.42 us: shards(): lax.all_gather(tokens, 'tensor', axis=1, tiled=True)]
    convert_element_type x2 -> x0, local copies, waits for them, and re-layouts: 9.34 us -> none  [the longest x1 4.68 us: shards(): back_terms.astype(jnp.bfloat16)]
  transfers between devices with their start and end apart: 5 -> 0, of which waited for: 5 -> 0; matrix products, arithmetic and copies ran while one was open for 7% -> 0% of each run, Pallas kernels for 0% -> 0%
where the time goes in v1:
time: 148 us
  Pallas kernels  140 us (95%)
  local copies, waits for them, and re-layouts  7.77 us (5%)
    pallas_call x1, Pallas kernels, shards(): pl.pallas_call(kernel, out_shape=(jax.ShapeDtypeStruct(tokens.shape, BF),...  140 us
    unnamed x6, local copies, waits for them, and re-layouts  7.77 us

profile of v1, /device:TPU:1, one launch (start us, length us, event | category | flops | bytes accessed | tf_op | source)
XLA Modules:
  0.0 148.1 jit_solution(13252895346472095142)
XLA Ops:
  0.6 139.7 %shard_map.84 = (bf16[256,256]{1,0:T(8,128)(2,1)}, bf16[256,256]{1,0:T(8,128)(2,1)}, bf16[8,8,128,128]{3,2,1,0:T(8,128)(2,1)}, bf16[8,8,128,128]{3,2,1,0:T(8,128)(2,1)}) custom-call(bf16[256,256]{1,0:T(8,128)(2,1)} %tokens.1, bf16[256,256]{1,0:T(8,128)(2,1)} %grads.1, s32[8,8]{1,0:T(8,128)} %pats.1, s32[8,8]{1,0:T(8,128)} %pats.1, ...), custom_call_target="tpu_custom_call" | custom-call | tf_op jit(solution)/shard_map/pallas_call | solution.py:539
  140.4 1.6 %copy.13 = bf16[256,256]{1,0:T(8,128)(2,1)} copy(bf16[256,256]{1,0:T(8,128)(2,1)} %get-tuple-element.8) | data formatting | bytes 262144
  141.9 1.6 %copy.14 = bf16[256,256]{1,0:T(8,128)(2,1)} copy(bf16[256,256]{1,0:T(8,128)(2,1)} %get-tuple-element.9) | data formatting | bytes 262144
  143.5 0.0 copy-start
  143.5 3.3 %copy.15 = bf16[8,8,128,128]{3,2,1,0:T(8,128)(2,1)} copy(bf16[8,8,128,128]{3,2,1,0:T(8,128)(2,1)} %get-tuple-element.10) | data formatting | bytes 4194304
  146.8 0.0 copy-done
  146.8 1.3 copy.16
Async XLA Ops:
  143.5 3.3 %copy-start = (bf16[8,8,128,128]{3,2,1,0:T(8,128)(2,1)S(1)}, bf16[8,8,128,128]{3,2,1,0:T(8,128)(2,1)}, u32[]{:S(2)}) copy-start(bf16[8,8,128,128]{3,2,1,0:T(8,128)(2,1)} %get-tuple-element.11) | copy-start | bytes 6291460

commit v2 on v1

v2 whole, which is shorter than its diff:
```python
import heapq

import jax
import jax.numpy as jnp
from jax import lax
from jax.experimental import pallas as pl
from jax.experimental.pallas import tpu as pltpu
from jax.sharding import PartitionSpec as P

MESH = pl.DeviceIdType.MESH
BF = jnp.bfloat16
F32 = jnp.float32

gelu_scale = 0.7978845608028654
gelu_cube = 0.044715

NX, NZ, NY = 4, 8, 4
ROWS, BLK, HR, K = 256, 128, 8, 8
RA = 96
RB = ROWS - RA
SIGNS = (1, -1)


OPT = dict(
    ra=(RA, RA, RA, RA), UNIT=2.7, LAT=1.9, g1=56, g2=66, g3=36, dzs=(4, 3, -3, 2, -2, 1, -1, 0), dxs=(2, 1, -1, 0),
    pf=0, ps=-1, cl=1.6, h=4, late_dz=(), late_dx=(0, 1, -1),
)
GROUP = {k: "ag" for k in ("ax", "az", "bz", "bx")} | {k: "rs" for k in ("rz", "rx", "sx", "sz")}
COST = {"ag": 0.03, "rs": 0.22}


def name(axis, s):
    return axis + ("+" if s > 0 else "-")


DZ=(4,3,-3,2,-2,1,-1,0)
def nz(dz): return 4 if dz==-4 else dz
def pair_of(key):
    if key[0]=="pc": return key
    if key[0]=="cg": return key[:2]
    return key[:-2]+key[-1:]
def recv_need(key):
    kind="out" if key[1]==0 else "back"
    if key[0] in ("rz","sz"): return [(kind, nz(c*(key[-1]-1))) for c in SIGNS]
    if key[0]=="rx": return [(kind,0)]
    if key[0]=="sx": return [(kind,key[2])]
    if key[0]=="pc": return [("grad",key[1],2)]
    return []
def build_items(o):
    items={}
    def add(key, link, size, deps): items[key]=(link,size,tuple(deps))
    for p in (0, 1):
        gate = [("gate", "ag", p)]
        fa = o["ra"][p] / ROWS
        fb = 1 - fa
        for s in SIGNS:
            add(("bz", p, s, 1), name("z", s), fb, gate)
            add(("ax", p, s, 1), name("x", s), fa, gate)
        for s in SIGNS:
            add(("az", p, 0, s, 1), name("z", s), fa, gate)
            add(("bx", p, 0, s, 1), name("x", s), fb, gate)
        for s in SIGNS:
            add(("ax", p, s, 2), name("x", s), fa / 2, [("ax", p, s, 1)])
            for k in (2, 3, 4):
                add(("bz", p, s, k), name("z", s), fb if k < 4 else fb / 2, [("bz", p, s, k - 1)])
        for dx, ready in ((0, gate),(-1, [("ax", p, 1, 1)]),(1, [("ax", p, -1, 1)]),(2, [("ax", p, 1, 2), ("ax", p, -1, 2)])):
            for s in SIGNS:
                for k in (1, 2, 3, 4):
                    add(("az", p, dx, s, k), name("z", s), fa if k < 4 else fa / 2, ready if k == 1 else [("az", p, dx, s, k - 1)])
        for dz in (0, -1, 1, -2, 2, -3, 3, 4):
            if dz == 0: ready = gate
            elif dz == 4: ready = [("bz", p, 1, 4), ("bz", p, -1, 4)]
            else: ready = [("bz", p, 1 if dz < 0 else -1, abs(dz))]
            for s in SIGNS:
                add(("bx", p, dz, s, 1), name("x", s), fb, ready)
                add(("bx", p, dz, s, 2), name("x", s), fb / 2, [("bx", p, dz, s, 1)])
    for q in (0, 1):
        kd="out" if q==0 else "back"
        fa = o["ra"][2 + q] / ROWS
        fb = 1 - fa
        def gate(c): return [("gate","rs",q)] + ([("gate2","rs",q)] if c else [])
        def done_a(dx): return [("rz", q, dx, s, 1) for s in SIGNS]
        def done_b(dz): return [("sx", q, dz, s, 1) for s in SIGNS]
        for dx in o["dxs"]:
            for s in SIGNS:
                for k in (4, 3, 2, 1):
                    add(("rz", q, dx, s, k), name("z", s), fa if k < 4 else fa / 2, (gate(dx in o.get("late_dx",())) if k == 4 else [("rz", q, dx, s, k + 1)])+[(kd,nz(s*k))])
        for dz in o["dzs"]:
            for s in SIGNS:
                add(("sx", q, dz, s, 2), name("x", s), fb / 2, gate(dz in o.get("late_dz",()))+[(kd,dz)])
                add(("sx", q, dz, s, 1), name("x", s), fb, [("sx", q, dz, s, 2)])
        for s in SIGNS:
            add(("rx", q, s, 2), name("x", s), fa / 2, done_a(2))
            add(("rx", q, s, 1), name("x", s), fa, [("rx", q, s, 2)] + done_a(s))
            add(("sz", q, s, 4), name("z", s), fb / 2, done_b(4))
            for k in (3, 2, 1):
                add(("sz", q, s, k), name("z", s), fb, [("sz", q, s, k + 1)] + done_b(s * k))
    for m in (0, 1):
        for v in (0,1):
            add(("pc", m, v), "c", o["cl"]/2, [("grad", m, v)])
        pcs=[("pc",m,0),("pc",m,1),("grad",m,2)]
        for u in (0,1):
            for s in SIGNS:
                add(("yr", m, u, s, 2), name("y", s), 0.5, pcs)
                add(("yr", m, u, s, 1), name("y", s), 1.0, [("yr", m, u, s, 2)])
        for u in (0,1):
            fin = [("yr", m, u, s, 1) for s in SIGNS]
            for s in SIGNS:
                add(("yg", m, u, s, 1), name("y", s), 1.0, fin)
                add(("yg", m, u, s, 2), name("y", s), 0.5, [("yg", m, u, s, 1)])
            add(("cg", m, u, 0), "c", 0.2, fin)
            add(("cg", m, u, -1), "c", 0.2, [("yg", m, u, 1, 1)])
            add(("cg", m, u, 1), "c", 0.2, [("yg", m, u, -1, 1)])
            add(("cg", m, u, 2), "c", 0.2, [("yg", m, u, 1, 2), ("yg", m, u, -1, 2)])
    return items
def build_chunks(o, items):
    def all_of(kinds, p): return [k for k in items if k[0] in kinds and k[1] == p]
    ag = ("ax", "az", "bz", "bx")
    chunks = [(("load",), 0.3, [("count", "ag", 0, 30)])]
    chunks += [(("pre", i), 0.56, all_of(ag, 0) + [("load",)]) for i in range(4)]
    pre = [("pre", i) for i in range(4)]
    chunks += [(("out", dz), 1.25, pre) for dz in o["dzs"]]
    agr = [("agrad", i) for i in range(4)]
    tail=[(("back",dz),1.33,agr) for dz in o["dzs"]]
    ft=[(("fterm",i),.63,agr) for i in range(4)]
    st=[(("sterm",i),.5,all_of(ag,1)+pre) for i in range(4)]
    tail[o["pf"]:o["pf"]]=ft
    ps=o["ps"]
    if ps>=0: tail[ps:ps]=st
    ag_=[(("agrad",i),.55,all_of(ag,1)+pre) for i in range(4)]
    chunks += (st if ps<0 else [])+ag_+tail
    return chunks
def build_marks(o, items):
    final = [[("rx", q, s, 1) for s in SIGNS]+ [("rz", q, 0, s, 1) for s in SIGNS]+ [("sz", q, s, 1) for s in SIGNS]+ [("sx", q, 0, s, 1) for s in SIGNS] for q in (0, 1)]
    marks = [
        (("gate", "ag", 0), []),
        (("gate", "ag", 1), [("count", "ag", 0, o["g1"])]),
        (("gate", "rs", 0), [("count", "ag", 1, o["g2"])]),
        (("gate", "rs", 1), [("count", "rs", 0, o["g3"])]),
        (("gate2", "rs", 0), [("count", "rs", 0, o.get("h",0))]),
        (("gate2", "rs", 1), [("count", "rs", 1, o.get("h",0))]),
        (("store", 0), final[0]),(("store", 1), final[1]),
    ]
    for m,n in ((0,"sterm"),(1,"fterm")):
        marks += [(("grad", m, 0), [(n,0)]),(("grad", m, 1), [(n,1)]),(("grad", m, 2), [(n,i) for i in range(4)])]
        for u in (0,1): marks.append((("own",m,u),[("yr",m,u,s,1) for s in SIGNS]))
    return marks
def build_order(o):
    items = build_items(o); chunks = build_chunks(o, items); marks = build_marks(o, items)
    UNIT,LAT=o["UNIT"],o["LAT"]
    got, counts, free = set(), {}, {}
    waiting = list(items); heap, order = [], []; now, seq = 0.0, 0
    pend={}; members={}
    for k in items: members[pair_of(k)]=members.get(pair_of(k),0)+1
    def met(need):
        if need[0] == "count": return counts.get((need[1], need[2]), 0) >= need[3]
        return need in got
    def settle():
        nonlocal now, seq
        moved = True
        while moved:
            moved = False
            for mark in list(marks):
                if all(met(n) for n in mark[1]):
                    marks.remove(mark); order.append(("mark", mark[0])); got.add(mark[0]); moved = True
            for key in list(waiting):
                link, size, deps = items[key]
                if all(d in got for d in deps):
                    waiting.remove(key); order.append(("send", key)); now += 0.03
                    start = max(now, free.get(link, 0.0))
                    free[link] = start + size * UNIT; seq += 1
                    pair=pair_of(key); pend.setdefault(pair,[]).append(free[link]+LAT)
                    if len(pend[pair])==members[pair]: heapq.heappush(heap, (max(pend[pair]), seq, pair))
                    moved = True
    settle()
    held=[]
    while heap or chunks or held:
        key=None
        for h in held:
            if all(n in got for n in recv_need(h)): key=h; held.remove(h); break
        if key is None and heap and heap[0][0] <= now:
            key = heapq.heappop(heap)[2]
            if not all(n in got for n in recv_need(key)): held.append(key); continue
        if key is not None:
            order.append(("recv", key)); got.update(k for k in items if pair_of(k)==key)
            group = GROUP.get(key[0], "ar"); counts[(group, key[1])] = counts.get((group, key[1]), 0) + members[key]
            now += COST.get(group, 0.2); settle(); continue
        if chunks and all(met(n) for n in chunks[0][2]):
            key, time, _ = chunks.pop(0); order.append(("comp", key)); got.add(key); now += time
            settle(); continue
        if not heap: return None
        now = max(now, heap[0][0])
    if waiting or marks: return None
    return list(items), order, now


KEYS, ORDER, SPAN = build_order(OPT)
PAIRS = list(dict.fromkeys(pair_of(k) for k in KEYS))
INDEX = {k: i for i, k in enumerate(PAIRS)}


def slot_index():
    a, b, y = {}, {}, {}
    na = nb = ny = 0
    for k in PAIRS:
        split = k[-1] == (4 if k[0][-1] == "z" else 2)
        n = 1 if split else 2
        if k[0] in ("rz", "rx") and k[1] == 0:
            a[(k[0],) + k[2:]] = na
            na += n
        if k[0] in ("sx", "sz") and k[1] == 0:
            b[(k[0],) + k[2:]] = nb
            nb += n
        if k[0] == "yr" and k[1:3] == (0, 0):
            y[k[-1]] = ny
            ny += n
    return a, b, y, na, nb, ny


SLOT_A, SLOT_B, SLOT_Y, NA, NB, NYS = slot_index()
SENT = {"ag": (0, 1), "rs": (0, 1), "ar": (0, 1)}
SEND = {"ag": 0, "rs": 2, "pc": 4, "yr": 4, "yg": 6, "cg": 6}


def gelu_pair(value):
    inner = gelu_scale * (value + gelu_cube * value * value * value)
    tangent = jnp.tanh(inner)
    result = 0.5 * value * (1.0 + tangent)
    slope = 0.5 * (1.0 + tangent) + 0.5 * value * (1.0 - tangent * tangent) * gelu_scale * (
        1.0 + 3.0 * gelu_cube * value * value
    )
    return result, slope


def kernel(
    tokens, grads, patv, pats, first, second,
    out_ref, back_ref, fgrad_ref, sgrad_ref,
    xb, gb, part0, part1, slot_a, slot_b, w1, w2, act, pgrad, slope_ref,
    sgr, fgr, pair, yslot, invv, invs,
    send_sem, recv_sem, local_sem,
):
    t = lax.axis_index("tensor")
    d = lax.axis_index("dp")
    x, z = lax.div(t, NZ), lax.rem(t, NZ)
    y, core = lax.div(d, 2), lax.rem(d, 2)

    def at(dx, dz):
        return lax.rem(x + (dx + NX), NX) * NZ + lax.rem(z + (dz + NZ), NZ)

    def dev_x(s):
        return {"tensor": at(s, 0)}

    def dev_z(s):
        return {"tensor": at(0, s)}

    def dev_y(s):
        return {"dp": lax.rem(y + (s + NY), NY) * 2 + core}

    partner = {"dp": y * 2 + (1 - core)}
    base = core * 4

    def yrow(dy, b=None):
        return (base if b is None else b) + lax.rem(y + (dy + NY), NY)

    barrier = pltpu.get_barrier_semaphore()
    for dev in (dev_x(1), dev_x(-1), dev_z(1), dev_z(-1), dev_y(1), dev_y(-1), partner):
        pl.semaphore_signal(barrier, inc=1, device_id=dev, device_id_type=MESH)

    local = []
    for n, (src, buf) in enumerate(((tokens, xb), (grads, gb))):
        for h in (0, 1):
            c = pltpu.make_async_copy(
                src.at[:, pl.ds(h * BLK, BLK)], buf.at[t, h], local_sem.at[2 * n + h]
            )
            c.start()
            local.append(c)
    load_w1 = pltpu.make_async_copy(first, w1.at[:, pl.ds(0, K)], local_sem.at[4])
    load_w2 = pltpu.make_async_copy(second, w2.at[:, pl.ds(0, K)], local_sem.at[5])
    load_w1.start()
    load_w2.start()

    cols = lax.broadcasted_iota(jnp.int32, (HR, BLK), 1)
    inv = jnp.full((HR, BLK), K, jnp.int32)
    for j in range(K):
        inv = jnp.where(patv[:, j : j + 1] == cols, j, inv)
    invv[...] = inv
    load_inv = pltpu.make_async_copy(invv, invs, local_sem.at[6])
    load_inv.start()
    for c in local:
        c.wait()

    pl.semaphore_wait(barrier, 7)

    gathered = (xb, gb)
    parts = (part0, part1)
    grad_of = (sgr, fgr)
    grad_out = (sgrad_ref, fgrad_ref)
    rows_a, rows_b = pl.ds(0, RA), pl.ds(RA, RB)

    def half(s):
        return 0 if s > 0 else 1

    def reduce_slot(key):
        kind, q, s, k = key[0], key[1], key[-2], key[-1]
        sub = (kind,) + key[2:-2] + (k,)
        split = k == (4 if kind[1] == "z" else 2)
        lane = 0 if split or s > 0 else 1
        if kind[0] == "r":
            return rows_a, slot_a.at[q, SLOT_A[sub] + lane], split
        return rows_b, slot_b.at[q, SLOT_B[sub] + lane], split

    def reduce_shard(key, k):
        kind, s = key[0], key[-2]
        if kind == "rz":
            return at(key[2], s * k)
        if kind == "sz":
            return at(0, s * k)
        if kind == "rx":
            return at(s * k, 0)
        return at(s * k, key[2])

    def copy_of(key):
        kind, p = key[0], key[1]
        group = GROUP.get(kind, kind)
        ss, rs = send_sem.at[SEND[group] + p], recv_sem.at[INDEX[pair_of(key)]]

        def remote(src, dst, dev):
            return pltpu.make_async_remote_copy(
                src_ref=src, dst_ref=dst, send_sem=ss, recv_sem=rs, device_id=dev, device_id_type=MESH
            )

        if group == "ag":
            s, k = key[-2], key[-1]
            rows = rows_a if kind[0] == "a" else rows_b
            if kind == "ax":
                own, dev, split = at(-s * (k - 1), 0), dev_x(s), k == 2
            elif kind == "az":
                own, dev, split = at(key[2], -s * (k - 1)), dev_z(s), k == 4
            elif kind == "bz":
                own, dev, split = at(0, -s * (k - 1)), dev_z(s), k == 4
            else:
                own, dev, split = at(-s * (k - 1), key[2]), dev_x(s), k == 2
            view = gathered[p].at[own, pl.ds(half(s), 1) if split else pl.ds(0, 2), rows, :]
            return remote(view, view, dev)
        if group == "rs":
            s, k = key[-2], key[-1]
            rows, slot, split = reduce_slot(key)
            hs = pl.ds(half(s), 1) if split else pl.ds(0, 2)
            dev = dev_z(s) if kind[1] == "z" else dev_x(s)
            return remote(parts[p].at[reduce_shard(key, k), hs, rows, :], slot.at[hs], dev)
        g, out = grad_of[p], grad_out[p]
        if kind == "pc":
            v = key[2] * 2
            return remote(g.at[pl.ds((1 - core) * 4 + v, 2)], pair.at[p, pl.ds(v, 2)], partner)
        u, s, k = key[2] * 4, key[-2], key[-1]
        if kind == "cg":
            js, dy = pl.ds(u, 4), key[3]
            src = g.at[yrow(0), js] if dy == 0 else out.at[yrow(dy), js]
            return remote(src, out.at[yrow(dy), js], partner)
        js = pl.ds(u + half(s) * 2, 2) if k == 2 else pl.ds(u, 4)
        if kind == "yr":
            slot = SLOT_Y[k] + (0 if k == 2 or s > 0 else 1)
            return remote(g.at[yrow(s * k), js], yslot.at[p, slot, js], dev_y(s))
        src = g.at[yrow(0), js] if k == 1 else out.at[yrow(-s), js]
        return remote(src, out.at[yrow(-s * (k - 1)), js], dev_y(s))

    def wait_for(view, sem, sent=False):
        c = pltpu.make_async_remote_copy(
            src_ref=view, dst_ref=view, send_sem=sem, recv_sem=sem, device_id=partner, device_id_type=MESH
        )
        if sent:
            c.wait_send()
        else:
            c.wait_recv()

    def received(key):
        kind, p = key[0], key[1]
        sem = recv_sem.at[INDEX[key]]
        group = GROUP.get(kind, kind)
        if group == "ag":
            rows = rows_a if kind[0] == "a" else rows_b
            split = key[-1] == (4 if kind[1] == "z" else 2)
            wait_for(gathered[p].at[pl.ds(0, 1 if split else 2), :, rows, :], sem)
        elif group == "rs":
            split = key[-1] == (4 if kind[1] == "z" else 2)
            signed = [key[:-1] + (s, key[-1]) for s in SIGNS]
            rows = rows_a if kind[0] == "r" else rows_b
            wait_for(parts[p].at[pl.ds(0, 1 if split else 2), :, rows, :], sem)
            places = [reduce_shard(k, key[-1] - 1) for k in signed]
            slots = [reduce_slot(k)[1] for k in signed]
            if key[-1] == 1:
                for h in (0, 1):
                    total = parts[p][places[0], h, rows, :].astype(F32)
                    total = total + slots[0][h].astype(F32) + slots[1][h].astype(F32)
                    parts[p][places[0], h, rows, :] = total.astype(BF)
                return
            for s, mine, slot in zip(SIGNS, places, slots):
                for h in (half(s),) if split else (0, 1):
                    total = parts[p][mine, h, rows, :].astype(F32) + slot[h].astype(F32)
                    parts[p][mine, h, rows, :] = total.astype(BF)
        elif kind == "pc":
            v = key[2] * 2
            g = grad_of[p]
            wait_for(pair.at[p, pl.ds(v, 2)], sem)

            @pl.loop(v, v + 2)
            def _(r):
                @pl.loop(0, K)
                def _(j):
                    total = g[base + r, j].astype(F32) + pair[p, r, j].astype(F32)
                    g[base + r, j] = total.astype(BF)
        elif kind == "yr":
            u, k = key[2] * 4, key[-1]
            g = grad_of[p]
            if k == 2:
                wait_for(yslot.at[p, SLOT_Y[2], pl.ds(u, 4)], sem)
                for s in SIGNS:
                    row = yrow(s)
                    lo = u + half(s) * 2

                    @pl.loop(lo, lo + 2)
                    def _(j):
                        total = g[row, j].astype(F32) + yslot[p, SLOT_Y[2], j].astype(F32)
                        g[row, j] = total.astype(BF)
            else:
                wait_for(yslot.at[p, pl.ds(SLOT_Y[1], 2), pl.ds(u, 4)], sem)
                row = yrow(0)

                @pl.loop(u, u + 4)
                def _(j):
                    total = g[row, j].astype(F32) + yslot[p, SLOT_Y[1], j].astype(F32)
                    total = total + yslot[p, SLOT_Y[1] + 1, j].astype(F32)
                    g[row, j] = total.astype(BF)
        elif kind == "yg":
            wait_for(grad_out[p].at[pl.ds(0, 2 if key[-1] == 1 else 1), pl.ds(key[2] * 4, 4)], sem)
        else:
            wait_for(grad_out[p].at[pl.ds(0, 4)], sem)

    def picked(buf, r):
        return jnp.concatenate([buf[lax.div(pats[r, j], 2), lax.rem(pats[r, j], 2)] for j in range(K)], axis=1)

    def whole(ref):
        return jnp.concatenate([ref[r] for r in range(HR)], axis=1)

    nt = (((1,), (1,)), ((), ()))

    def compute(key):
        kind = key[0]
        if kind == "load":
            load_w1.wait()
            load_w2.wait()
            load_inv.wait()
            for w in (w1, w2):
                for r in range(HR):
                    w[r, K] = jnp.zeros((BLK, BLK), BF)
            return
        i = key[1]
        if kind in ("out", "back"):

            @pl.loop(0, NX)
            def _(dx):
                dest = lax.rem(x + dx, NX) * NZ + lax.rem(z + (i + NZ), NZ)
                if kind == "out":
                    rhs = jnp.concatenate(
                        [
                            jnp.concatenate([w2[r, invs[r, 2 * dest + h]] for r in range(HR)], axis=0)
                            for h in (0, 1)
                        ],
                        axis=1,
                    )
                    res = jnp.dot(whole(act), rhs, preferred_element_type=F32)
                else:
                    rhs = jnp.concatenate(
                        [
                            jnp.concatenate([w1[r, invs[r, 2 * dest + h]] for r in range(HR)], axis=1)
                            for h in (0, 1)
                        ],
                        axis=0,
                    )
                    res = lax.dot_general(whole(pgrad), rhs, nt, preferred_element_type=F32)
                buf = part0 if kind == "out" else part1
                for h in (0, 1):
                    buf[dest, h] = res[:, h * BLK : (h + 1) * BLK].astype(BF)

            return

        @pl.loop(i * 2, i * 2 + 2)
        def _(n):
            r = lax.rem((1 - core) * 4 + n, HR)
            if kind == "pre":
                weights = jnp.concatenate([w1[r, j] for j in range(K)], axis=0)
                pre = jnp.dot(picked(xb, r), weights, preferred_element_type=F32)
                value, slope = gelu_pair(pre)
                act[r] = value.astype(BF)
                slope_ref[r] = slope
            elif kind == "sterm":
                res = jnp.dot(act[r].T, picked(gb, r), preferred_element_type=F32)
                for j in range(K):
                    sgr[r, j] = res[:, j * BLK : (j + 1) * BLK].astype(BF)
            elif kind == "agrad":
                weights = jnp.concatenate([w2[r, j] for j in range(K)], axis=1)
                res = lax.dot_general(picked(gb, r), weights, nt, preferred_element_type=F32)
                pgrad[r] = (res * slope_ref[r]).astype(BF)
            elif kind == "fterm":
                res = jnp.dot(pgrad[r].T, picked(xb, r), preferred_element_type=F32)
                for j in range(K):
                    fgr[r, j] = res[:, j * BLK : (j + 1) * BLK].astype(BF).T

    stores = []

    def store(src, dst):
        c = pltpu.make_async_copy(src, dst, local_sem.at[8 + len(stores)])
        c.start()
        stores.append(c)

    def marked(key):
        if key[0] == "store":
            q = key[1]
            dst = (out_ref, back_ref)[q]
            for h in (0, 1):
                store(parts[q].at[t, h], dst.at[:, pl.ds(h * BLK, BLK)])
        elif key[0] == "own":
            m, js = key[1], pl.ds(key[2] * 4, 4)
            store(grad_of[m].at[yrow(0), js], grad_out[m].at[yrow(0), js])

    for action, key in ORDER:
        if action == "send":
            copy_of(key).start()
        elif action == "recv":
            received(key)
        elif action == "comp":
            compute(key)
        else:
            marked(key)
    for p in (0, 1):
        if p in SENT["ag"]:
            wait_for(gathered[p].at[pl.ds(0, 31)], send_sem.at[SEND["ag"] + p], True)
        if p in SENT["rs"]:
            wait_for(parts[p].at[pl.ds(0, 31)], send_sem.at[SEND["rs"] + p], True)
        if p in SENT["ar"]:
            wait_for(grad_of[p].at[pl.ds(0, 7)], send_sem.at[SEND["yr"] + p], True)
            wait_for(grad_of[p].at[pl.ds(0, 7)], send_sem.at[SEND["yg"] + p], True)
    for c in stores:
        c.wait()


def finish(*refs):
    srcs, dsts, sem = refs[:4], refs[4:8], refs[8]
    copies = [pltpu.make_async_copy(src, dst, sem.at[i]) for i, (src, dst) in enumerate(zip(srcs, dsts))]
    for c in copies:
        c.start()
    for c in copies:
        c.wait()


def shards(tokens, pattern, first_blocks, second_blocks, out_grad):
    any_space = pl.BlockSpec(memory_space=pltpu.HBM)
    n = len(PAIRS)
    shapes = (
            jax.ShapeDtypeStruct(tokens.shape, BF),
            jax.ShapeDtypeStruct(tokens.shape, BF),
            jax.ShapeDtypeStruct(first_blocks.shape, BF),
            jax.ShapeDtypeStruct(second_blocks.shape, BF),
        )
    results = pl.pallas_call(
        kernel,
        out_shape=tuple(pltpu.VMEM(r.shape, BF) for r in shapes),
        in_specs=[
            any_space,
            any_space,
            pl.BlockSpec(memory_space=pltpu.VMEM),
            pl.BlockSpec(memory_space=pltpu.SMEM),
            any_space,
            any_space,
        ],
        out_specs=(pl.BlockSpec(memory_space=pltpu.VMEM),) * 4,
        scratch_shapes=[
            pltpu.VMEM((32, 2, ROWS, BLK), BF),
            pltpu.VMEM((32, 2, ROWS, BLK), BF),
            pltpu.VMEM((32, 2, ROWS, BLK), BF),
            pltpu.VMEM((32, 2, ROWS, BLK), BF),
            pltpu.VMEM((2, NA, 2, RA, BLK), BF),
            pltpu.VMEM((2, NB, 2, RB, BLK), BF),
            pltpu.VMEM((HR, K + 1, BLK, BLK), BF),
            pltpu.VMEM((HR, K + 1, BLK, BLK), BF),
            pltpu.VMEM((HR, ROWS, BLK), BF),
            pltpu.VMEM((HR, ROWS, BLK), BF),
            pltpu.VMEM((HR, ROWS, BLK), F32),
            pltpu.VMEM((HR, K, BLK, BLK), BF),
            pltpu.VMEM((HR, K, BLK, BLK), BF),
            pltpu.VMEM((2, 4, K, BLK, BLK), BF),
            pltpu.VMEM((2, NYS, K, BLK, BLK), BF),
            pltpu.VMEM((HR, BLK), jnp.int32),
            pltpu.SMEM((HR, BLK), jnp.int32),
            pltpu.SemaphoreType.DMA((8,)),
            pltpu.SemaphoreType.DMA((n,)),
            pltpu.SemaphoreType.DMA((16,)),
        ],
        compiler_params=pltpu.CompilerParams(
            collective_id=0, has_side_effects=True, vmem_limit_bytes=62500000
        ),
    )(tokens, out_grad, pattern, pattern, first_blocks, second_blocks)
    return pl.pallas_call(
        finish,
        out_shape=shapes,
        in_specs=[pl.BlockSpec(memory_space=pltpu.VMEM)] * 4,
        out_specs=(any_space,) * 4,
        scratch_shapes=[pltpu.SemaphoreType.DMA((4,))],
        compiler_params=pltpu.CompilerParams(vmem_limit_bytes=4 * 1024 * 1024),
    )(*[pltpu.with_memory_space_constraint(r, pltpu.VMEM) for r in results])


def solution(mesh):
    placed = (
        P("dp", "tensor"),
        P("tensor", None),
        P("tensor", None, None, None),
        P("tensor", None, None, None),
        P("dp", "tensor"),
    )
    return jax.shard_map(
        shards,
        mesh=mesh,
        in_specs=placed,
        out_specs=(
            P("dp", "tensor"),
            P("dp", "tensor"),
            P("tensor", None, None, None),
            P("tensor", None, None, None),
        ),
        check_vma=False,
    )
```

time: 148 us -> 116 us (0.78)
  Pallas kernels: 140 us -> 116 us
  local copies, waits for them, and re-layouts: 7.77 us -> 0 us
    pallas_call x1 -> x2, Pallas kernels: 140 us -> 116 us  [the longest x1 114 us: shards(): pl.pallas_call(kernel, out_shape=tuple((pltpu.VMEM(r.shape, BF) for r in...]
    unnamed x6 -> x0, local copies, waits for them, and re-layouts: 7.77 us -> none
where the time goes in v2:
time: 116 us
  Pallas kernels  116 us (100%)
    pallas_call x1, Pallas kernels, shards(): pl.pallas_call(kernel, out_shape=tuple((pltpu.VMEM(r.shape, BF) for r in...  114 us

profile of v2, /device:TPU:1, one launch (start us, length us, event | category | flops | bytes accessed | tf_op | source)
XLA Modules:
  0.0 116.3 jit_solution(6932062759868723698)
XLA Ops:
  0.6 113.5 %shard_map.84 = (bf16[256,256]{1,0:T(8,128)(2,1)S(1)}, bf16[256,256]{1,0:T(8,128)(2,1)S(1)}, bf16[8,8,128,128]{3,2,1,0:T(8,128)(2,1)S(1)}, bf16[8,8,128,128]{3,2,1,0:T(8,128)(2,1)S(1)}) custom-call(bf16[256,256]{1,0:T(8,128)(2,1)} %tokens.1, bf16[256,256]{1,0:T(8,128)(2,1)} %grads.1, s32[8,8]{1,0:T(8,128)} %pats.1, s32[8,8]{1,0:T(8,128)} %pats.1, ...), custom_call_target="tpu_custom_call" | custom-call | tf_op jit(solution)/shard_map/pallas_call | solution.py:565
  114.1 2.1 %shard_map.85 = (bf16[256,256]{1,0:T(8,128)(2,1)}, bf16[256,256]{1,0:T(8,128)(2,1)}, bf16[8,8,128,128]{3,2,1,0:T(8,128)(2,1)}, bf16[8,8,128,128]{3,2,1,0:T(8,128)(2,1)}) custom-call(bf16[256,256]{1,0:T(8,128)(2,1)S(1)} %get-tuple-element.8.refs_0_, bf16[256,256]{1,0:T(8,128)(2,1)S(1)} %get-tuple-element.9.refs_1_, ...), custom_call_target="tpu_custom_call" | custom-call | tf_op jit(solution)/shard_map/pallas_call | solution.py:603

commit v3 on v2

--- a/solution.py
+++ b/solution.py
@@ -16,15 +16,30 @@
 
 NX, NZ, NY = 4, 8, 4
 ROWS, BLK, HR, K = 256, 128, 8, 8
-RA = 96
-RB = ROWS - RA
 SIGNS = (1, -1)
 
 
 OPT = dict(
-    ra=(RA, RA, RA, RA), UNIT=2.7, LAT=1.9, g1=56, g2=66, g3=36, dzs=(4, 3, -3, 2, -2, 1, -1, 0), dxs=(2, 1, -1, 0),
-    pf=0, ps=-1, cl=1.6, h=4, late_dz=(), late_dx=(0, 1, -1),
+    ra=(96, 112, 112, 96),
+    UNIT=2.75,
+    LAT=2.5,
+    TH=1.5,
+    PH=30,
+    y=0.93,
+    g1=8,
+    g2=52,
+    g3=60,
+    dzs=(4, 3, -3, 2, -2, 1, -1, 0),
+    dxs=(2, 1, -1, 0),
+    pf=0,
+    ps=-1,
+    cl=0.8,
+    h=4,
+    late_dx=(0,),
+    late_dz=(0, 1, -1),
 )
+SPLIT = OPT["ra"]
+RA, RB = max(SPLIT), ROWS - min(SPLIT)
 GROUP = {k: "ag" for k in ("ax", "az", "bz", "bx")} | {k: "rs" for k in ("rz", "rx", "sx", "sz")}
 COST = {"ag": 0.03, "rs": 0.22}
 
@@ -145,12 +160,24 @@
         marks += [(("grad", m, 0), [(n,0)]),(("grad", m, 1), [(n,1)]),(("grad", m, 2), [(n,i) for i in range(4)])]
         for u in (0,1): marks.append((("own",m,u),[("yr",m,u,s,1) for s in SIGNS]))
     return marks
+def ranks(o, items):
+    after={}
+    for k,(_,_,deps) in items.items():
+        for d in deps: after.setdefault(d,[]).append(k)
+    left={}
+    def way(k):
+        if k not in left: left[k]=items[k][1]*o["UNIT"]+o["LAT"]+max([way(n) for n in after.get(k,[])]+[0.0])
+        return left[k]
+    def phase(k):
+        g=GROUP.get(k[0],"ar")
+        return k[1] if g=="ag" else 2+k[1] if g=="rs" else k[1]
+    return {k:(phase(k)*o["PH"]-way(k),i) for i,k in enumerate(items)}
 def build_order(o):
     items = build_items(o); chunks = build_chunks(o, items); marks = build_marks(o, items)
     UNIT,LAT=o["UNIT"],o["LAT"]
     got, counts, free = set(), {}, {}
     waiting = list(items); heap, order = [], []; now, seq = 0.0, 0
-    pend={}; members={}
+    pend={}; members={}; ready=[]; rank=ranks(o, items)
     for k in items: members[pair_of(k)]=members.get(pair_of(k),0)+1
     def met(need):
         if need[0] == "count": return counts.get((need[1], need[2]), 0) >= need[3]
@@ -164,11 +191,15 @@
                 if all(met(n) for n in mark[1]):
                     marks.remove(mark); order.append(("mark", mark[0])); got.add(mark[0]); moved = True
             for key in list(waiting):
-                link, size, deps = items[key]
-                if all(d in got for d in deps):
-                    waiting.remove(key); order.append(("send", key)); now += 0.03
+                if all(d in got for d in items[key][2]):
+                    waiting.remove(key); ready.append(key)
+            ready.sort(key=lambda k: rank[k])
+            for key in list(ready):
+                link, size, _ = items[key]
+                if free.get(link, 0.0) - now < o["TH"]:
+                    ready.remove(key); order.append(("send", key)); now += 0.03
                     start = max(now, free.get(link, 0.0))
-                    free[link] = start + size * UNIT; seq += 1
+                    free[link] = start + size * UNIT * o.get(link[0], 1.0); seq += 1
                     pair=pair_of(key); pend.setdefault(pair,[]).append(free[link]+LAT)
                     if len(pend[pair])==members[pair]: heapq.heappush(heap, (max(pend[pair]), seq, pair))
                     moved = True
@@ -190,7 +221,7 @@
             settle(); continue
         if not heap: return None
         now = max(now, heap[0][0])
-    if waiting or marks: return None
+    if waiting or marks or ready: return None
     return list(items), order, now
 
 
@@ -279,14 +310,8 @@
     load_w1.start()
     load_w2.start()
 
-    cols = lax.broadcasted_iota(jnp.int32, (HR, BLK), 1)
-    inv = jnp.full((HR, BLK), K, jnp.int32)
-    for j in range(K):
-        inv = jnp.where(patv[:, j : j + 1] == cols, j, inv)
-    invv[...] = inv
     load_inv = pltpu.make_async_copy(invv, invs, local_sem.at[6])
-    load_inv.start()
-    for c in local:
+    for c in local[:2]:
         c.wait()
 
     pl.semaphore_wait(barrier, 7)
@@ -295,19 +320,23 @@
     parts = (part0, part1)
     grad_of = (sgr, fgr)
     grad_out = (sgrad_ref, fgrad_ref)
-    rows_a, rows_b = pl.ds(0, RA), pl.ds(RA, RB)
+
+    def rows_of(key):
+        n = SPLIT[key[1] + (0 if GROUP[key[0]] == "ag" else 2)]
+        return (pl.ds(0, n), n) if key[0][0] in "ar" else (pl.ds(n, ROWS - n), ROWS - n)
 
     def half(s):
         return 0 if s > 0 else 1
 
     def reduce_slot(key):
+        rows, n = rows_of(key)
         kind, q, s, k = key[0], key[1], key[-2], key[-1]
         sub = (kind,) + key[2:-2] + (k,)
         split = k == (4 if kind[1] == "z" else 2)
         lane = 0 if split or s > 0 else 1
         if kind[0] == "r":
-            return rows_a, slot_a.at[q, SLOT_A[sub] + lane], split
-        return rows_b, slot_b.at[q, SLOT_B[sub] + lane], split
+            return rows, slot_a.at[q, SLOT_A[sub] + lane, :, pl.ds(0, n), :], split
+        return rows, slot_b.at[q, SLOT_B[sub] + lane, :, pl.ds(0, n), :], split
 
     def reduce_shard(key, k):
         kind, s = key[0], key[-2]
@@ -331,7 +360,7 @@
 
         if group == "ag":
             s, k = key[-2], key[-1]
-            rows = rows_a if kind[0] == "a" else rows_b
+            rows = rows_of(key)[0]
             if kind == "ax":
                 own, dev, split = at(-s * (k - 1), 0), dev_x(s), k == 2
             elif kind == "az":
@@ -378,13 +407,13 @@
         sem = recv_sem.at[INDEX[key]]
         group = GROUP.get(kind, kind)
         if group == "ag":
-            rows = rows_a if kind[0] == "a" else rows_b
+            rows = rows_of(key)[0]
             split = key[-1] == (4 if kind[1] == "z" else 2)
             wait_for(gathered[p].at[pl.ds(0, 1 if split else 2), :, rows, :], sem)
         elif group == "rs":
             split = key[-1] == (4 if kind[1] == "z" else 2)
             signed = [key[:-1] + (s, key[-1]) for s in SIGNS]
-            rows = rows_a if kind[0] == "r" else rows_b
+            rows = rows_of(key)[0]
             wait_for(parts[p].at[pl.ds(0, 1 if split else 2), :, rows, :], sem)
             places = [reduce_shard(k, key[-1] - 1) for k in signed]
             slots = [reduce_slot(k)[1] for k in signed]
@@ -447,6 +476,12 @@
     def compute(key):
         kind = key[0]
         if kind == "load":
+            cols = lax.broadcasted_iota(jnp.int32, (HR, BLK), 1)
+            inv = jnp.full((HR, BLK), K, jnp.int32)
+            for j in range(K):
+                inv = jnp.where(patv[:, j : j + 1] == cols, j, inv)
+            invv[...] = inv
+            load_inv.start()
             load_w1.wait()
             load_w2.wait()
             load_inv.wait()
@@ -514,6 +549,9 @@
         stores.append(c)
 
     def marked(key):
+        if key == ("gate", "ag", 1):
+            for c in local[2:]:
+                c.wait()
         if key[0] == "store":
             q = key[1]
             dst = (out_ref, back_ref)[q]

time: 116 us -> 110 us (0.948)
  Pallas kernels: 116 us -> 109 us
    pallas_call x1, Pallas kernels: 114 us -> 107 us  [shards(): pl.pallas_call(kernel, out_shape=tuple((pltpu.VMEM(r.shape, BF) for r in...]
where the time goes in v3:
time: 110 us
  Pallas kernels  109 us (99%)
    pallas_call x1, Pallas kernels, shards(): pl.pallas_call(kernel, out_shape=tuple((pltpu.VMEM(r.shape, BF) for r in...  107 us

profile of v3, /device:TPU:1, one launch (start us, length us, event | category | flops | bytes accessed | tf_op | source)
XLA Modules:
  0.0 110.0 jit_solution(13018228019965146617)
XLA Ops:
  0.6 107.2 %shard_map.84 = (bf16[256,256]{1,0:T(8,128)(2,1)S(1)}, bf16[256,256]{1,0:T(8,128)(2,1)S(1)}, bf16[8,8,128,128]{3,2,1,0:T(8,128)(2,1)S(1)}, bf16[8,8,128,128]{3,2,1,0:T(8,128)(2,1)S(1)}) custom-call(bf16[256,256]{1,0:T(8,128)(2,1)} %tokens.1, bf16[256,256]{1,0:T(8,128)(2,1)} %grads.1, s32[8,8]{1,0:T(8,128)} %pats.1, s32[8,8]{1,0:T(8,128)} %pats.1, ...), custom_call_target="tpu_custom_call" | custom-call | tf_op jit(solution)/shard_map/pallas_call | solution.py:603
  107.9 2.1 %shard_map.85 = (bf16[256,256]{1,0:T(8,128)(2,1)}, bf16[256,256]{1,0:T(8,128)(2,1)}, bf16[8,8,128,128]{3,2,1,0:T(8,128)(2,1)}, bf16[8,8,128,128]{3,2,1,0:T(8,128)(2,1)}) custom-call(bf16[256,256]{1,0:T(8,128)(2,1)S(1)} %get-tuple-element.8.refs_0_, bf16[256,256]{1,0:T(8,128)(2,1)S(1)} %get-tuple-element.9.refs_1_, ...), custom_call_target="tpu_custom_call" | custom-call | tf_op jit(solution)/shard_map/pallas_call | solution.py:641

commit v4 on v3

--- a/solution.py
+++ b/solution.py
@@ -1,4 +1,5 @@
 import heapq
+import random
 
 import jax
 import jax.numpy as jnp
@@ -20,15 +21,18 @@
 
 
 OPT = dict(
-    ra=(96, 112, 112, 96),
+    ra=(80, 112, 112, 96),
     UNIT=2.75,
     LAT=2.5,
     TH=1.5,
-    PH=30,
+    PH=20,
+    np=2,
+    seed=2803,
+    amp=0,
     y=0.93,
     g1=8,
-    g2=52,
-    g3=60,
+    g2=56,
+    g3=40,
     dzs=(4, 3, -3, 2, -2, 1, -1, 0),
     dxs=(2, 1, -1, 0),
     pf=0,
@@ -36,12 +40,12 @@
     cl=0.8,
     h=4,
     late_dx=(0,),
-    late_dz=(0, 1, -1),
+    late_dz=(0, 1, -1, 2, -2),
 )
 SPLIT = OPT["ra"]
 RA, RB = max(SPLIT), ROWS - min(SPLIT)
 GROUP = {k: "ag" for k in ("ax", "az", "bz", "bx")} | {k: "rs" for k in ("rz", "rx", "sx", "sz")}
-COST = {"ag": 0.03, "rs": 0.22}
+COST = {"ag": 0.03, "rs": 0.16}
 
 
 def name(axis, s):
@@ -134,9 +138,9 @@
     chunks = [(("load",), 0.3, [("count", "ag", 0, 30)])]
     chunks += [(("pre", i), 0.56, all_of(ag, 0) + [("load",)]) for i in range(4)]
     pre = [("pre", i) for i in range(4)]
-    chunks += [(("out", dz), 1.25, pre) for dz in o["dzs"]]
+    np=o["np"]; chunks += [(("out", dz, c), 10.0/8/np, pre) for dz in o["dzs"] for c in range(np)]
     agr = [("agrad", i) for i in range(4)]
-    tail=[(("back",dz),1.33,agr) for dz in o["dzs"]]
+    tail=[(("back",dz,c),10.6/8/np,agr) for dz in o["dzs"] for c in range(np)]
     ft=[(("fterm",i),.63,agr) for i in range(4)]
     st=[(("sterm",i),.5,all_of(ag,1)+pre) for i in range(4)]
     tail[o["pf"]:o["pf"]]=ft
@@ -156,6 +160,8 @@
         (("gate2", "rs", 1), [("count", "rs", 1, o.get("h",0))]),
         (("store", 0), final[0]),(("store", 1), final[1]),
     ]
+    for kd in ("out","back"):
+        marks += [((kd,dz),[(kd,dz,c) for c in range(o["np"])]) for dz in DZ]
     for m,n in ((0,"sterm"),(1,"fterm")):
         marks += [(("grad", m, 0), [(n,0)]),(("grad", m, 1), [(n,1)]),(("grad", m, 2), [(n,i) for i in range(4)])]
         for u in (0,1): marks.append((("own",m,u),[("yr",m,u,s,1) for s in SIGNS]))
@@ -171,7 +177,8 @@
     def phase(k):
         g=GROUP.get(k[0],"ar")
         return k[1] if g=="ag" else 2+k[1] if g=="rs" else k[1]
-    return {k:(phase(k)*o["PH"]-way(k),i) for i,k in enumerate(items)}
+    rnd=random.Random(o["seed"])
+    return {k:(phase(k)*o["PH"]-way(k)+o["amp"]*rnd.random(),i) for i,k in enumerate(items)}
 def build_order(o):
     items = build_items(o); chunks = build_chunks(o, items); marks = build_marks(o, items)
     UNIT,LAT=o["UNIT"],o["LAT"]
@@ -227,7 +234,19 @@
 
 KEYS, ORDER, SPAN = build_order(OPT)
 PAIRS = list(dict.fromkeys(pair_of(k) for k in KEYS))
-INDEX = {k: i for i, k in enumerate(PAIRS)}
+
+
+def semaphore_index():
+    index, n = {}, {}
+    for k in PAIRS:
+        group = GROUP.get(k[0], "ar")
+        slot = (group, k[1] if group != "ar" else 0)
+        index[k] = n.get(slot, 0) + (76 if group == "ar" else 38 * k[1])
+        n[slot] = n.get(slot, 0) + 1
+    return index, max(index.values()) + 1
+
+
+INDEX, NSEM = semaphore_index()
 
 
 def slot_index():
@@ -264,10 +283,10 @@
 
 
 def kernel(
-    tokens, grads, patv, pats, first, second,
+    tokens, grads, pattern, first, second,
     out_ref, back_ref, fgrad_ref, sgrad_ref,
     xb, gb, part0, part1, slot_a, slot_b, w1, w2, act, pgrad, slope_ref,
-    sgr, fgr, pair, yslot, invv, invs,
+    sgr, fgr, pair, yslot, patv, pats, invv, invs,
     send_sem, recv_sem, local_sem,
 ):
     t = lax.axis_index("tensor")
@@ -307,6 +326,12 @@
             local.append(c)
     load_w1 = pltpu.make_async_copy(first, w1.at[:, pl.ds(0, K)], local_sem.at[4])
     load_w2 = pltpu.make_async_copy(second, w2.at[:, pl.ds(0, K)], local_sem.at[5])
+    load_pat = [
+        pltpu.make_async_copy(pattern, patv, local_sem.at[7]),
+        pltpu.make_async_copy(pattern, pats, local_sem.at[8]),
+    ]
+    for c in load_pat:
+        c.start()
     load_w1.start()
     load_w2.start()
 
@@ -425,8 +450,7 @@
                 return
             for s, mine, slot in zip(SIGNS, places, slots):
                 for h in (half(s),) if split else (0, 1):
-                    total = parts[p][mine, h, rows, :].astype(F32) + slot[h].astype(F32)
-                    parts[p][mine, h, rows, :] = total.astype(BF)
+                    parts[p][mine, h, rows, :] = parts[p][mine, h, rows, :] + slot[h]
         elif kind == "pc":
             v = key[2] * 2
             g = grad_of[p]
@@ -436,8 +460,8 @@
             def _(r):
                 @pl.loop(0, K)
                 def _(j):
-                    total = g[base + r, j].astype(F32) + pair[p, r, j].astype(F32)
-                    g[base + r, j] = total.astype(BF)
+                    total = g[base + r, j] + pair[p, r, j]
+                    g[base + r, j] = total
         elif kind == "yr":
             u, k = key[2] * 4, key[-1]
             g = grad_of[p]
@@ -449,8 +473,8 @@
 
                     @pl.loop(lo, lo + 2)
                     def _(j):
-                        total = g[row, j].astype(F32) + yslot[p, SLOT_Y[2], j].astype(F32)
-                        g[row, j] = total.astype(BF)
+                        total = g[row, j] + yslot[p, SLOT_Y[2], j]
+                        g[row, j] = total
             else:
                 wait_for(yslot.at[p, pl.ds(SLOT_Y[1], 2), pl.ds(u, 4)], sem)
                 row = yrow(0)
@@ -476,6 +500,8 @@
     def compute(key):
         kind = key[0]
         if kind == "load":
+            for c in load_pat:
+                c.wait()
             cols = lax.broadcasted_iota(jnp.int32, (HR, BLK), 1)
             inv = jnp.full((HR, BLK), K, jnp.int32)
             for j in range(K):
@@ -492,7 +518,9 @@
         i = key[1]
         if kind in ("out", "back"):
 
-            @pl.loop(0, NX)
+            per = NX // OPT["np"]
+
+            @pl.loop(key[2] * per, key[2] * per + per)
             def _(dx):
                 dest = lax.rem(x + dx, NX) * NZ + lax.rem(z + (i + NZ), NZ)
                 if kind == "out":
@@ -544,7 +572,7 @@
     stores = []
 
     def store(src, dst):
-        c = pltpu.make_async_copy(src, dst, local_sem.at[8 + len(stores)])
+        c = pltpu.make_async_copy(src, dst, local_sem.at[9 + len(stores)])
         c.start()
         stores.append(c)
 
@@ -556,7 +584,7 @@
             q = key[1]
             dst = (out_ref, back_ref)[q]
             for h in (0, 1):
-                store(parts[q].at[t, h], dst.at[:, pl.ds(h * BLK, BLK)])
+                dst[:, h * BLK : (h + 1) * BLK] = parts[q][t, h]
         elif key[0] == "own":
             m, js = key[1], pl.ds(key[2] * 4, 4)
             store(grad_of[m].at[yrow(0), js], grad_out[m].at[yrow(0), js])
@@ -593,7 +621,7 @@
 
 def shards(tokens, pattern, first_blocks, second_blocks, out_grad):
     any_space = pl.BlockSpec(memory_space=pltpu.HBM)
-    n = len(PAIRS)
+    n = NSEM
     shapes = (
             jax.ShapeDtypeStruct(tokens.shape, BF),
             jax.ShapeDtypeStruct(tokens.shape, BF),
@@ -606,8 +634,7 @@
         in_specs=[
             any_space,
             any_space,
-            pl.BlockSpec(memory_space=pltpu.VMEM),
-            pl.BlockSpec(memory_space=pltpu.SMEM),
+            any_space,
             any_space,
             any_space,
         ],
@@ -628,16 +655,18 @@
             pltpu.VMEM((HR, K, BLK, BLK), BF),
             pltpu.VMEM((2, 4, K, BLK, BLK), BF),
             pltpu.VMEM((2, NYS, K, BLK, BLK), BF),
+            pltpu.VMEM((HR, K), jnp.int32),
+            pltpu.SMEM((HR, K), jnp.int32),
             pltpu.VMEM((HR, BLK), jnp.int32),
             pltpu.SMEM((HR, BLK), jnp.int32),
             pltpu.SemaphoreType.DMA((8,)),
             pltpu.SemaphoreType.DMA((n,)),
-            pltpu.SemaphoreType.DMA((16,)),
+            pltpu.SemaphoreType.DMA((13,)),
         ],
         compiler_params=pltpu.CompilerParams(
             collective_id=0, has_side_effects=True, vmem_limit_bytes=62500000
         ),
-    )(tokens, out_grad, pattern, pattern, first_blocks, second_blocks)
+    )(tokens, out_grad, pattern, first_blocks, second_blocks)
     return pl.pallas_call(
         finish,
         out_shape=shapes,

time: 110 us -> 108 us (0.982)
  Pallas kernels: 109 us -> 107 us
    pallas_call x1, Pallas kernels: 107 us -> 105 us  [shards(): pl.pallas_call(kernel, out_shape=tuple((pltpu.VMEM(r.shape, BF) for r in...]
where the time goes in v4:
time: 108 us; the launch traced here: 107 us
  Pallas kernels  107 us (99%)
    pallas_call x1, Pallas kernels, shards(): pl.pallas_call(kernel, out_shape=tuple((pltpu.VMEM(r.shape, BF) for r in...  105 us

profile of v4, /device:TPU:1, one launch (start us, length us, event | category | flops | bytes accessed | tf_op | source)
XLA Modules:
  0.0 107.4 jit_solution(13524194329902103963)
XLA Ops:
  0.6 104.7 %shard_map.84 = (bf16[256,256]{1,0:T(8,128)(2,1)S(1)}, bf16[256,256]{1,0:T(8,128)(2,1)S(1)}, bf16[8,8,128,128]{3,2,1,0:T(8,128)(2,1)S(1)}, bf16[8,8,128,128]{3,2,1,0:T(8,128)(2,1)S(1)}) custom-call(bf16[256,256]{1,0:T(8,128)(2,1)} %tokens.1, bf16[256,256]{1,0:T(8,128)(2,1)} %grads.1, s32[8,8]{1,0:T(8,128)} %pattern.1, bf16[8,8,128,128]{3,2,1,0:T(8,128)(2,1)} %first.1, ...), custom_call_target="tpu_custom_call" | custom-call | tf_op jit(solution)/shard_map/pallas_call | solution.py:631
  105.3 2.1 %shard_map.85 = (bf16[256,256]{1,0:T(8,128)(2,1)}, bf16[256,256]{1,0:T(8,128)(2,1)}, bf16[8,8,128,128]{3,2,1,0:T(8,128)(2,1)}, bf16[8,8,128,128]{3,2,1,0:T(8,128)(2,1)}) custom-call(bf16[256,256]{1,0:T(8,128)(2,1)S(1)} %get-tuple-element.8.refs_0_, bf16[256,256]{1,0:T(8,128)(2,1)S(1)} %get-tuple-element.9.refs_1_, ...), custom_call_target="tpu_custom_call" | custom-call | tf_op jit(solution)/shard_map/pallas_call | solution.py:670

commit v5 on v4

--- a/solution.py
+++ b/solution.py
@@ -25,22 +25,22 @@
     UNIT=2.75,
     LAT=2.5,
     TH=1.5,
-    PH=20,
-    np=2,
-    seed=2803,
-    amp=0,
+    PH=30,
+    np=1,
+    seed=4972,
+    amp=4,
     y=0.93,
-    g1=8,
-    g2=56,
-    g3=40,
+    g1=4,
+    g2=52,
+    g3=32,
     dzs=(4, 3, -3, 2, -2, 1, -1, 0),
     dxs=(2, 1, -1, 0),
     pf=0,
     ps=-1,
     cl=0.8,
-    h=4,
-    late_dx=(0,),
-    late_dz=(0, 1, -1, 2, -2),
+    h=16,
+    late_dx=(),
+    late_dz=(0,),
 )
 SPLIT = OPT["ra"]
 RA, RB = max(SPLIT), ROWS - min(SPLIT)

time: 108 us -> 107 us (level)
  no operation moved by 1% of the time
where the time goes in v5:
time: 107 us
  Pallas kernels  107 us (100%)
    pallas_call x1, Pallas kernels, shards(): pl.pallas_call(kernel, out_shape=tuple((pltpu.VMEM(r.shape, BF) for r in...  104 us

profile of v5, /device:TPU:1, one launch (start us, length us, event | category | flops | bytes accessed | tf_op | source)
XLA Modules:
  0.0 107.1 jit_solution(9364032249249011199)
XLA Ops:
  0.6 104.4 %shard_map.84 = (bf16[256,256]{1,0:T(8,128)(2,1)S(1)}, bf16[256,256]{1,0:T(8,128)(2,1)S(1)}, bf16[8,8,128,128]{3,2,1,0:T(8,128)(2,1)S(1)}, bf16[8,8,128,128]{3,2,1,0:T(8,128)(2,1)S(1)}) custom-call(bf16[256,256]{1,0:T(8,128)(2,1)} %tokens.1, bf16[256,256]{1,0:T(8,128)(2,1)} %grads.1, s32[8,8]{1,0:T(8,128)} %pattern.1, bf16[8,8,128,128]{3,2,1,0:T(8,128)(2,1)} %first.1, ...), custom_call_target="tpu_custom_call" | custom-call | tf_op jit(solution)/shard_map/pallas_call | solution.py:631
  105.0 2.1 %shard_map.85 = (bf16[256,256]{1,0:T(8,128)(2,1)}, bf16[256,256]{1,0:T(8,128)(2,1)}, bf16[8,8,128,128]{3,2,1,0:T(8,128)(2,1)}, bf16[8,8,128,128]{3,2,1,0:T(8,128)(2,1)}) custom-call(bf16[256,256]{1,0:T(8,128)(2,1)S(1)} %get-tuple-element.8.refs_0_, bf16[256,256]{1,0:T(8,128)(2,1)S(1)} %get-tuple-element.9.refs_1_, ...), custom_call_target="tpu_custom_call" | custom-call | tf_op jit(solution)/shard_map/pallas_call | solution.py:670

commit v6 on v5

--- a/solution.py
+++ b/solution.py
@@ -312,17 +312,14 @@
     def yrow(dy, b=None):
         return (base if b is None else b) + lax.rem(y + (dy + NY), NY)
 
-    barrier = pltpu.get_barrier_semaphore()
-    for dev in (dev_x(1), dev_x(-1), dev_z(1), dev_z(-1), dev_y(1), dev_y(-1), partner):
-        pl.semaphore_signal(barrier, inc=1, device_id=dev, device_id_type=MESH)
-
     local = []
     for n, (src, buf) in enumerate(((tokens, xb), (grads, gb))):
         for h in (0, 1):
             c = pltpu.make_async_copy(
                 src.at[:, pl.ds(h * BLK, BLK)], buf.at[t, h], local_sem.at[2 * n + h]
             )
-            c.start()
+            if n == 0:
+                c.start()
             local.append(c)
     load_w1 = pltpu.make_async_copy(first, w1.at[:, pl.ds(0, K)], local_sem.at[4])
     load_w2 = pltpu.make_async_copy(second, w2.at[:, pl.ds(0, K)], local_sem.at[5])
@@ -330,16 +327,18 @@
         pltpu.make_async_copy(pattern, patv, local_sem.at[7]),
         pltpu.make_async_copy(pattern, pats, local_sem.at[8]),
     ]
-    for c in load_pat:
-        c.start()
-    load_w1.start()
-    load_w2.start()
 
     load_inv = pltpu.make_async_copy(invv, invs, local_sem.at[6])
+    barrier = pltpu.get_barrier_semaphore()
+    for dev in (dev_x(1), dev_x(-1), dev_z(1), dev_z(-1), dev_y(1), dev_y(-1), partner):
+        pl.semaphore_signal(barrier, inc=1, device_id=dev, device_id_type=MESH)
+
+
     for c in local[:2]:
         c.wait()
-
     pl.semaphore_wait(barrier, 7)
+    for c in local[2:] + load_pat + [load_w1, load_w2]:
+        c.start()
 
     gathered = (xb, gb)
     parts = (part0, part1)

time: 107 us -> 107 us (level)
  no operation moved by 1% of the time
where the time goes in v6:
time: 107 us
  Pallas kernels  107 us (100%)
    pallas_call x1, Pallas kernels, shards(): pl.pallas_call(kernel, out_shape=tuple((pltpu.VMEM(r.shape, BF) for r in...  104 us

profile of v6, /device:TPU:1, one launch (start us, length us, event | category | flops | bytes accessed | tf_op | source)
XLA Modules:
  0.0 107.1 jit_solution(8056427197334880020)
XLA Ops:
  0.6 104.4 %shard_map.84 = (bf16[256,256]{1,0:T(8,128)(2,1)S(1)}, bf16[256,256]{1,0:T(8,128)(2,1)S(1)}, bf16[8,8,128,128]{3,2,1,0:T(8,128)(2,1)S(1)}, bf16[8,8,128,128]{3,2,1,0:T(8,128)(2,1)S(1)}) custom-call(bf16[256,256]{1,0:T(8,128)(2,1)} %tokens.1, bf16[256,256]{1,0:T(8,128)(2,1)} %grads.1, s32[8,8]{1,0:T(8,128)} %pattern.1, bf16[8,8,128,128]{3,2,1,0:T(8,128)(2,1)} %first.1, ...), custom_call_target="tpu_custom_call" | custom-call | tf_op jit(solution)/shard_map/pallas_call | solution.py:630
  105.0 2.1 %shard_map.85 = (bf16[256,256]{1,0:T(8,128)(2,1)}, bf16[256,256]{1,0:T(8,128)(2,1)}, bf16[8,8,128,128]{3,2,1,0:T(8,128)(2,1)}, bf16[8,8,128,128]{3,2,1,0:T(8,128)(2,1)}) custom-call(bf16[256,256]{1,0:T(8,128)(2,1)S(1)} %get-tuple-element.8.refs_0_, bf16[256,256]{1,0:T(8,128)(2,1)S(1)} %get-tuple-element.9.refs_1_, ...), custom_call_target="tpu_custom_call" | custom-call | tf_op jit(solution)/shard_map/pallas_call | solution.py:669
